TPU v7x, 128 devices: a whole 4x4x4 slice. The times are simulated.
128 devices in a mesh: det: 16 (over z_lo, x, core), strip: 8 (over y, z_hi).
Axes of the slice: x: 4, y: 4, z: 4 (z_hi: 2, z_lo: 2; z = z_hi * 2 + z_lo), core: 2. Of those that a mesh axis runs over, the one named last changes fastest.
Arguments:
- science: float32 [16, 256, 4096], P('det', 'strip'), may hold values from -17 to 17
- template: float32 [16, 256, 4096], P(None, 'strip', 'det'), may hold values from -8 to 8
- row_taps: float32 [12, 21], replicated, may hold values from -1.25 to 1.25
- col_taps: float32 [12, 21], replicated, may hold values from -1.25 to 1.25
- stamp_rows: int32 [16, 32], P('det'), may hold values from 17 to 238
- stamp_cols: int32 [16, 32], P('det'), may hold values from 17 to 4078
Outputs:
- difference: float32 [16, 256, 4096], P('det', 'strip')
- kernel_coeffs: float32 [16, 37], P('det')
All inputs are finite; a program needn't handle non-finite values.
Results may differ from a plain program's by a relative error of at most 0.0003.
Values sent between devices are 32-bit elements; how exact they have to be, the bound alone decides.
A program may use at most 128 MiB of HBM per device.

v0:
```python
import jax
import jax.numpy as jnp
from jax import lax
from jax.sharding import PartitionSpec as P

NB = 12
KS = 21
HS = 17
KH = 10
NU = 37


RIDGE_WEIGHT = 1.0
HIGHEST_MODE = lax.Precision.HIGHEST
LANE_WIDTH = 128


def padded_2(block, sides, width):
    for axis, dim in sides:
        count = lax.axis_size(axis)
        forward = [(i, i + 1) for i in range(count - 1)]
        backward = [(target, source) for source, target in forward]
        low = lax.ppermute(
            lax.slice_in_dim(block, block.shape[dim] - width, None, axis=dim), axis, forward
        )
        high = lax.ppermute(lax.slice_in_dim(block, 0, width, axis=dim), axis, backward)
        block = jnp.concatenate([low, block, high], axis=dim)
    return block


def column_tables(col_taps):
    offset = jnp.arange(2 * LANE_WIDTH)[:, None] - jnp.arange(LANE_WIDTH)[None, :]
    onehot = (offset[None] == jnp.arange(KS)[:, None, None]).astype(jnp.float32)
    whole = jnp.einsum("bv,vij->bij", col_taps, onehot, precision=HIGHEST_MODE)
    return (whole[:, :LANE_WIDTH, :], whole[:, LANE_WIDTH:, :])


def row_table(row_taps, row_count):
    offset = jnp.arange(row_count + 2 * KH)[None, :] - jnp.arange(row_count)[:, None]
    onehot = (offset[None] == jnp.arange(KS)[:, None, None]).astype(jnp.float32)
    return jnp.einsum("bv,vyk->byk", row_taps, onehot, precision=HIGHEST_MODE)


def correlate(framed, main_tab, next_tab, row_tab):
    depth, col_count = framed.shape
    col_blocks = col_count // LANE_WIDTH
    padded = jnp.pad(framed, ((0, 0), (KH, LANE_WIDTH - KH)))
    central = padded[:, :col_count].reshape(depth, col_blocks, LANE_WIDTH)
    following = padded[:, LANE_WIDTH : col_count + LANE_WIDTH].reshape(
        depth, col_blocks, LANE_WIDTH
    )
    across = jnp.einsum("rki,bij->brkj", central, main_tab, precision=HIGHEST_MODE)
    across = across + jnp.einsum("rki,bij->brkj", following, next_tab, precision=HIGHEST_MODE)
    across = across.reshape(NB, depth, col_count)
    return jnp.einsum("byk,bkc->byc", row_tab, across, precision=HIGHEST_MODE)


def apply_model(responses, coeffs, y_coord, x_coord):
    base_part = jnp.tensordot(coeffs[:NB], responses, axes=1, precision=HIGHEST_MODE)
    x_part = jnp.tensordot(coeffs[NB : 2 * NB], responses, axes=1, precision=HIGHEST_MODE)
    y_part = jnp.tensordot(coeffs[2 * NB : 3 * NB], responses, axes=1, precision=HIGHEST_MODE)
    return base_part + x_coord * x_part + y_coord * y_part + coeffs[NU - 1]


def local(science, template, row_taps, col_taps, stamp_rows, stamp_cols):
    det_count, row_count, col_count = science.shape
    moved = lax.all_to_all(template, "det", split_axis=0, concat_axis=2, tiled=True)
    framed = padded_2(moved, (("strip", 1),), KH)
    total_rows = row_count * lax.axis_size("strip")
    first_global = lax.axis_index("strip") * row_count
    global_rows = first_global + jnp.arange(row_count, dtype=jnp.int32)
    y_coord = (2.0 * global_rows.astype(jnp.float32) / total_rows - 1.0)[:, None]
    col_index = jnp.arange(col_count, dtype=jnp.int32)
    x_coord = (2.0 * col_index.astype(jnp.float32) / col_count - 1.0)[None, :]
    main_tab, next_tab = column_tables(col_taps)
    row_tab = row_table(row_taps, row_count)
    y_flat = jnp.broadcast_to(y_coord, (row_count, col_count)).reshape(1, -1)
    x_flat = jnp.broadcast_to(x_coord, (row_count, col_count)).reshape(1, -1)
    unity = jnp.ones((1, row_count * col_count), jnp.float32)
    responses = correlate(framed[0], main_tab, next_tab, row_tab)
    observed = science[0]
    row_hits = (jnp.abs(global_rows[:, None] - stamp_rows[0][None, :]) <= HS).astype(jnp.float32)
    col_hits = (jnp.abs(stamp_cols[0][:, None] - col_index[None, :]) <= HS).astype(jnp.float32)
    weight = jnp.dot(
        row_hits, col_hits, precision=HIGHEST_MODE, preferred_element_type=jnp.float32
    ).reshape(1, -1)
    flat = responses.reshape(NB, -1)
    feats = jnp.concatenate([flat, flat * x_flat, flat * y_flat, unity], axis=0)
    weighted = feats * weight
    normal = jnp.einsum("ip,jp->ij", weighted, feats, precision=HIGHEST_MODE)
    target = jnp.einsum("ip,p->i", weighted, observed.reshape(-1), precision=HIGHEST_MODE)
    normal, target = lax.psum((normal, target), "strip")
    normal = normal + RIDGE_WEIGHT * jnp.eye(NU, dtype=jnp.float32)
    factor = jnp.linalg.cholesky(normal)
    coeffs = jax.scipy.linalg.cho_solve((factor, True), target)
    differences = [observed - apply_model(responses, coeffs, y_coord, x_coord)]
    solutions = [coeffs]
    return (jnp.stack(differences), jnp.stack(solutions))


def solution(mesh):
    return jax.shard_map(
        local,
        mesh=mesh,
        in_specs=(
            P("det", "strip", None),
            P(None, "strip", "det"),
            P(),
            P(),
            P("det", None),
            P("det", None),
        ),
        out_specs=(P("det", "strip", None), P("det", None)),
        check_vma=False,
    )
```

profile of v0, /device:TPU:0, one launch (start us, length us, event | category | flops | bytes accessed | tf_op | source)
XLA Modules:
  0.0 230.8 jit_solution(16646424460032151319)
XLA Ops:
  0.7 6.0 %all-to-all-start = ((f32[16,32,256]{2,1,0:T(8,128)}), f32[16,32,256]{2,1,0:T(8,128)}, u32[]{:S(2)}, u32[]{:S(2)}) async-start(f32[16,32,256]{2,1,0:T(8,128)} %param.7), calls=%async_computation | async-start | bytes 1048576 | tf_op jit(solution)/shard_map/all_to_all | solution.py:67
  6.8 0.1 broadcast_bitcast_fusion
  6.9 0.1 copy.35
  7.0 0.1 copy.34
  7.1 1.0 convolution_bitcast_fusion
  8.2 0.9 copy.36
  9.1 2.4 %copy.37 = f32[1,1,32,4096]{3,1,2,0:T(1,128)} copy(f32[1,1,32,4096]{3,2,1,0:T(8,128)} %bitcast.123) | data formatting | bytes 1048576
  11.4 1.4 fusion.15
  12.8 0.1 pad.8.clone
  13.0 0.1 slice_bitcast_fusion
  13.1 4.5 %all-to-all-done = f32[16,32,256]{2,1,0:T(8,128)} async-done(((f32[16,32,256]{2,1,0:T(8,128)}), f32[16,32,256]{2,1,0:T(8,128)}, u32[]{:S(2)}, u32[]{:S(2)}) %all-to-all-start) | async-done | bytes 524320 | tf_op jit(solution)/shard_map/all_to_all | solution.py:67
  17.6 1.1 copy.30
  18.7 5.5 %collective-permute-start = (f32[1,10,4096]{2,1,0:T(8,128)S(1)}, f32[1,10,4096]{2,1,0:T(8,128)S(1)}, u32[]{:S(2)}, u32[]{:S(2)}) collective-permute-start(f32[1,10,4096]{2,1,0:T(8,128)S(1)} %get-tuple-element.10), channel_id=1, source_target_pairs={{0,1},{1,2},{2,3},{3,4},{4,5},{5,6},{6,7},{8,9},{9,10},{10,11},{11... | collective-permute-start | bytes 491528 | tf_op jit(solution)/shard_map/ppermute | solution.py:23
  24.3 1.5 collective-permute-start.1
  25.7 0.3 fusion.32
  26.0 9.0 %collective-permute-done = f32[1,10,4096]{2,1,0:T(8,128)S(1)} collective-permute-done((f32[1,10,4096]{2,1,0:T(8,128)S(1)}, f32[1,10,4096]{2,1,0:T(8,128)S(1)}, u32[]{:S(2)}, u32[]{:S(2)}) %collective-permute-start) | collective-permute-done | bytes 163872 | tf_op jit(solution)/shard_map/ppermute | solution.py:23
  35.0 0.0 collective-permute-done.1
  35.0 0.1 maximum_bitcast_fusion
  35.1 0.5 pad_slice_fusion
  35.6 0.2 copy.31
  35.8 0.1 slice.63
  35.9 0.2 copy.32
  36.1 0.1 slice.64
  36.1 9.2 %fusion.21 = f32[12,128,52,32]{1,2,3,0:T(8,128)S(1)} fusion(f32[52,32,128]{2,1,0:T(8,128)S(1)} %slice.63, f32[12,128,128,1]{2,0,1,3:T(8,128)S(1)} %get-tuple-element.7), kind=kOutput, calls=%fused_computation.29 | convolution fusion | flops 3925868544 | bytes 11862016 | tf_op jit(solution)/shard_map/rki,bij->brkj/dot_general | solution.py:52
  45.3 10.5 %add_bitcast_fusion = f32[12,52,32,128]{3,1,2,0:T(8,128)S(1)} fusion(f32[12,128,52,32]{1,2,3,0:T(8,128)S(1)} %fusion.21, f32[52,32,128]{2,1,0:T(8,128)S(1)} %slice.64, f32[12,128,128,1]{2,0,1,3:T(8,128)S(1)} %get-tuple-element.6), kind=kOutput, calls=%fused_computation.5 | convolution fusion | flops 3928424448 | bytes 22085632 | tf_op jit(solution)/shard_map/rki,bij->brkj/dot_general | solution.py:53
  55.9 5.5 %copy.16 = f32[12,52,32,128]{3,2,1,0:T(8,128)} copy(f32[12,52,32,128]{3,1,2,0:T(8,128)S(1)} %add_bitcast_fusion) | data formatting | bytes 20447232 | tf_op jit(solution)/shard_map/add | solution.py:53
  61.4 10.2 %reshape.85 = f32[12,52,4096]{2,1,0:T(8,128)} reshape(f32[12,52,32,128]{3,2,1,0:T(8,128)} %copy.16) | data formatting | bytes 20447232 | tf_op jit(solution)/shard_map/reshape | solution.py:54
  71.6 9.3 %fusion.36 = f32[12,32,4096]{2,1,0:T(8,128)S(1)} fusion(f32[12,52,4096]{2,1,0:T(8,128)} %reshape.85, f32[32,52,12]{1,2,0:T(8,128)S(1)} %fusion.32), kind=kOutput, calls=%fused_computation.52 | convolution fusion | flops 981467136 | bytes 16594944 | tf_op jit(solution)/shard_map/byk,bkc->byc/dot_general | solution.py:55
  80.9 2.7 %copy-done.2 = f32[12,32,4096]{2,1,0:T(8,128)} copy-done((f32[12,32,4096]{2,1,0:T(8,128)}, f32[12,32,4096]{2,1,0:T(8,128)S(1)}, u32[]{:S(2)}) %copy-start.2) | copy-done | bytes 6291480
  83.6 0.9 pad.12
  84.5 4.9 %copy.33 = f32[2,8,32,4096]{3,1,2,0:T(8,128)S(1)} copy(f32[2,8,32,4096]{3,2,1,0:T(8,128)S(1)} %bitcast.116) | data formatting | bytes 16777216
  89.4 6.6 %broadcast_multiply_fusion.1 = (f32[12,131072]{1,0:T(8,128)}, f32[12,131072]{1,0:T(8,128)}) fusion(f32[12,131072]{1,0:T(8,128)S(1)} %bitcast.113, f32[131072]{0:T(1024)S(1)} %bitcast.125, f32[131072]{0:T(1024)S(1)} %bitcast.124), kind=kLoop, calls=%fused_computation.17 | loop fusion | flops 3145728 | bytes 19922944 | tf_op jit(solution)/shard_map/mul | solution.py:88
  96.0 1.6 copy-done.3
  97.6 26.7 %fusion.2 = f32[37,37]{1,0:T(8,128)S(1)} fusion(f32[12,131072]{1,0:T(8,128)} %get-tuple-element.5, f32[12,131072]{1,0:T(8,128)} %get-tuple-element.4, f32[12,131072]{1,0:T(8,128)} %bitcast.114, f32[37]{0:T(128)S(1)} %pad.8.clone, f32[131072]{0:T(1024)S(1)} %bitcast.126), kind=kOutput, calls=%fused_computation.2 | convolution fusion | flops 2187198464 | bytes 19404280 | tf_op jit(solution)/shard_map/ip,jp->ij/dot_general | solution.py:90
  124.4 21.7 %fusion.17 = f32[37]{0:T(128)S(1)} fusion(f32[131072,1]{0,1:T(1,128)S(1)} %bitcast.128, f32[12,131072]{1,0:T(8,128)} %get-tuple-element.5, f32[12,131072]{1,0:T(8,128)} %get-tuple-element.4, f32[12,131072]{1,0:T(8,128)} %bitcast.115, f32[37]{0:T(128)S(1)} %pad.8.clone, f32[131072]{0:T(1024)S(1)} %bitcast.127), kind=kOutput, calls=%fused_computation.23 | convolution fusion | flops 77594624 | bytes 19923240 | tf_op jit(solution)/shard_map/ip,p->i/dot_general | solution.py:91
  146.0 41.4 %all-reduce.1 = (f32[37,37]{1,0:T(8,128)S(1)}, f32[37]{0:T(128)S(1)}) all-reduce(f32[37,37]{1,0:T(8,128)S(1)} %fusion.2, f32[37]{0:T(128)S(1)} %fusion.17), channel_id=1, replica_groups=mesh['det'=16,'strip'=8] {'strip'}, use_global_device_ids=true, to_apply=%region_0.1 | all-reduce | flops 1406 | bytes 11248 | tf_op jit(solution)/shard_map/psum | solution.py:92
  187.4 0.1 copy.17
  187.5 3.4 %cholesky.17 = f32[37,37]{1,0:T(8,128)S(1)} custom-call(f32[37,37]{1,0:T(8,128)S(1)} %fusion.43), custom_call_target="Cholesky" | custom-call | tf_op jit(solution)/shard_map/jit(cholesky)/cholesky | solution.py:94
  190.9 0.6 compare_reduce_fusion
  191.6 0.7 fusion.39
  192.2 2.8 %custom-call.10 = f32[1,37,37]{1,2,0:T(8,128)S(1)} custom-call(f32[1,37,37]{2,1,0:T(8,128)S(1)} %fusion.39), custom_call_target="InvertDiagBlocksLowerTriangular" | custom-call | tf_op jit(solution)/shard_map/jit(_cho_solve)/triangular_solve | solution.py:95
  195.1 0.2 convolution_bitcast_fusion.1
  195.2 0.1 fusion.40
  195.4 11.3 %fusion.12 = f32[1,32,4096]{2,0,1:T(1,128)S(1)} fusion(f32[12,32,4096]{2,1,0:T(8,128)} %copy-done.2, f32[37]{0:T(128)S(1)} %bitcast.129), kind=kOutput, calls=%fused_computation.14 | convolution fusion | flops 18874368 | bytes 6815892 | tf_op jit(solution)/shard_map/dot_general | solution.py:59
  206.8 11.4 %fusion.10 = f32[1,32,4096]{2,0,1:T(1,128)S(1)} fusion(f32[12,32,4096]{2,1,0:T(8,128)} %copy-done.2, f32[37]{0:T(128)S(1)} %bitcast.130), kind=kOutput, calls=%fused_computation.12 | convolution fusion | flops 18874368 | bytes 6815892 | tf_op jit(solution)/shard_map/dot_general | solution.py:60
  218.2 9.3 %fusion.8 = f32[1,32,4096]{2,0,1:T(1,128)S(1)} fusion(f32[12,32,4096]{2,1,0:T(8,128)S(1)} %bitcast.112, f32[37]{0:T(128)S(1)} %bitcast.131), kind=kOutput, calls=%fused_computation.10 | convolution fusion | flops 18874368 | bytes 6815892 | tf_op jit(solution)/shard_map/dot_general | solution.py:61
  227.4 0.6 slice.58
  228.0 2.5 %fusion.30 = f32[1,32,4096]{2,1,0:T(8,128)} fusion(f32[1,32,4096]{2,1,0:T(8,128)S(1)} %copy-done.4, f32[1,32,4096]{2,0,1:T(1,128)S(1)} %fusion.8, f32[1,32,4096]{2,0,1:T(1,128)S(1)} %fusion.10, f32[1,32,4096]{2,0,1:T(1,128)S(1)} %fusion.12, f32[]{:T(128)} %bitcast.29, f32[32]{0:T(128)S(1)} %multiply_add_fusion.1, f32[4096]{0:T(1024)S(1)} %multiply_add_fusion), kind=kLoop, calls=%fused_computation.41 | loop fusion | flops 786432 | bytes 2637956 | tf_op jit(solution)/shard_map/stack | solution.py:98
  (32 shorter events, 0.3 us)
Async XLA Ops:
  0.6 10.8 %copy-start = (f32[12,21]{1,0:T(8,128)S(1)}, f32[12,21]{1,0:T(8,128)}, u32[]{:S(2)}) copy-start(f32[12,21]{1,0:T(8,128)} %param.9) | copy-start | bytes 3028
  0.6 25.1 %copy-start.8 = (f32[12,21]{1,0:T(8,128)S(1)}, f32[12,21]{1,0:T(8,128)}, u32[]{:S(2)}) copy-start(f32[12,21]{1,0:T(8,128)} %param.8) | copy-start | bytes 3028
  0.7 17.0 %all-to-all-start = ((f32[16,32,256]{2,1,0:T(8,128)}), f32[16,32,256]{2,1,0:T(8,128)}, u32[]{:S(2)}, u32[]{:S(2)}) async-start(f32[16,32,256]{2,1,0:T(8,128)} %param.7), calls=%async_computation | async-start | bytes 1048576 | tf_op jit(solution)/shard_map/all_to_all | solution.py:67
  18.7 16.3 %collective-permute-start = (f32[1,10,4096]{2,1,0:T(8,128)S(1)}, f32[1,10,4096]{2,1,0:T(8,128)S(1)}, u32[]{:S(2)}, u32[]{:S(2)}) collective-permute-start(f32[1,10,4096]{2,1,0:T(8,128)S(1)} %get-tuple-element.10), channel_id=1, source_target_pairs={{0,1},{1,2},{2,3},{3,4},{4,5},{5,6},{6,7},{8,9},{9,10},{10,11},{11... | collective-permute-start | bytes 491528 | tf_op jit(solution)/shard_map/ppermute | solution.py:23
  24.3 10.8 %collective-permute-start.1 = (f32[1,10,4096]{2,1,0:T(8,128)S(1)}, f32[1,10,4096]{2,1,0:T(8,128)S(1)}, u32[]{:S(2)}, u32[]{:S(2)}) collective-permute-start(f32[1,10,4096]{2,1,0:T(8,128)S(1)} %get-tuple-element.11), channel_id=1, source_target_pairs={{1,0},{2,1},{3,2},{4,3},{5,4},{6,5},{7,6},{9,8},{10,9},{11,10},{12... | collective-permute-start | bytes 491528 | tf_op jit(solution)/shard_map/ppermute | solution.py:26
  80.9 2.7 %copy-start.2 = (f32[12,32,4096]{2,1,0:T(8,128)}, f32[12,32,4096]{2,1,0:T(8,128)S(1)}, u32[]{:S(2)}) copy-start(f32[12,32,4096]{2,1,0:T(8,128)S(1)} %fusion.36) | copy-start | bytes 18874372
  89.4 8.3 %copy-start.3 = (f32[2,8,32,4096]{3,1,2,0:T(8,128)}, f32[2,8,32,4096]{3,1,2,0:T(8,128)S(1)}, u32[]{:S(2)}) copy-start(f32[2,8,32,4096]{3,1,2,0:T(8,128)S(1)} %copy.33) | copy-start | bytes 25165828
  89.4 8.3 %copy-start.5 = (f32[4,32,8,128]{3,1,2,0:T(8,128)S(1)}, f32[4,32,8,128]{3,1,2,0:T(8,128)}, u32[]{:S(2)}) copy-start(f32[4,32,8,128]{3,1,2,0:T(8,128)} %copy.36) | copy-start | bytes 1572868
  97.6 26.7 %copy-start.6 = (f32[1,1,32,4096]{3,1,2,0:T(1,128)S(1)}, f32[1,1,32,4096]{3,1,2,0:T(1,128)}, u32[]{:S(2)}) copy-start(f32[1,1,32,4096]{3,1,2,0:T(1,128)} %copy.37) | copy-start | bytes 1572868
  195.4 32.1 %copy-start.7 = (f32[1,37]{1,0:T(1,128)}, f32[1,37]{1,0:T(1,128)S(1)}, u32[]{:S(2)}) copy-start(f32[1,37]{1,0:T(1,128)S(1)} %fusion.40) | copy-start | bytes 448
  195.4 22.8 %slice-start = ((s8[6291456]{0:T(1024)(128)(4,1)}), s8[4194304]{0:T(1024)(128)(4,1)S(1)}, s32[]{:S(2)}) async-start(s8[6291456]{0:T(1024)(128)(4,1)} %bitcast.111), calls=%async_computation.1 | async-start | bytes 8388608
  195.4 35.2 %copy-start.1 = (f32[12,21]{1,0:T(8,128)S(1)}, f32[12,21]{1,0:T(8,128)}, u32[]{:S(2)}) copy-start(f32[12,21]{1,0:T(8,128)} %param.9) | copy-start | bytes 3028
  206.7 11.4 %slice-start.1 = ((s8[6291456]{0:T(1024)(128)(4,1)}), s8[2097152]{0:T(1024)(128)(4,1)S(1)}, s32[]{:S(2)}) async-start(s8[6291456]{0:T(1024)(128)(4,1)} %bitcast.111), calls=%async_computation.2 | async-start | bytes 4194304
  206.7 21.3 %copy-start.4 = (f32[1,32,4096]{2,1,0:T(8,128)S(1)}, f32[1,32,4096]{2,1,0:T(8,128)}, u32[]{:S(2)}) copy-start(f32[1,32,4096]{2,1,0:T(8,128)} %param.6) | copy-start | bytes 1572868
where the time goes:
time: 234 us; the launch traced here: 231 us
  matrix products  112 us (48%)
  blocking collectives  41.4 us (18%)
  local copies, waits for them, and re-layouts  32.4 us (14%)
  other arithmetic  16.9 us (7%)
  waiting for transfers between devices  13.5 us (6%)
  starting transfers between devices  13 us (6%)
    psum x1, blocking collectives, local(): normal, target = lax.psum((normal, target), 'strip')  41.4 us
    dot_general x1, matrix products, local(): normal = jnp.einsum('ip,jp->ij', weighted, feats, precision=HIGHEST_MODE)  26.7 us
    dot_general x1, matrix products, local(): jnp.einsum('ip,p->i', weighted, observed.reshape(-1), precision=HIGHEST_M...  21.7 us
    unnamed x32, local copies, waits for them, and re-layouts  14 us
    dot_general x1, matrix products, apply_model(): jnp.tensordot(coeffs[NB:2 * NB], responses, axes=1, precision=HIGHEST_MODE)  11.4 us
    dot_general x1, matrix products, apply_model(): jnp.tensordot(coeffs[:NB], responses, axes=1, precision=HIGHEST_MODE)  11.3 us
    dot_general x1, matrix products, correlate(): jnp.einsum('rki,bij->brkj', following, next_tab, precision=HIGHEST_MODE)  10.5 us
    reshape x1, local copies, waits for them, and re-layouts, correlate(): across = across.reshape(NB, depth, col_count)  10.2 us
  transfers between devices with their start and end apart: 3, of which 2 were waited for; matrix products, arithmetic and copies ran while one was open for 3% of the time, Pallas kernels for 0%

commit v1 on v0

v1 whole, which is shorter than its diff:
```python
import functools

import jax
import jax.numpy as jnp
from jax import lax
from jax.experimental import pallas as pl
from jax.experimental.pallas import tpu as pltpu
from jax.sharding import PartitionSpec as P

NB = 12
KS = 21
HS = 17
KH = 10
NU = 37
LW = 128
HALO = 16
SLOT = 42
PLANES = 16
ONE_PLANE = 12
SCI_PLANE = 13
RIDGE_WEIGHT = 1.0
HIGHEST_MODE = lax.Precision.HIGHEST
MESH = pl.DeviceIdType.MESH
BF = jnp.bfloat16
F32 = jnp.float32


def iota(shape, dim):
    return lax.broadcasted_iota(jnp.int32, shape, dim)


def split(value):
    high = value.astype(BF)
    return high, (value - high.astype(F32)).astype(BF)


def build_row_table(taps_ref, pad_ref, table_ref, rows):
    pad_ref[...] = jnp.zeros_like(pad_ref)
    pad_ref[:NB, :KS] = taps_ref[...]
    for b in range(NB):
        wide = jnp.broadcast_to(pad_ref[b : b + 1, :], (rows, LW))
        moved = pltpu.roll(wide, HALO - KH, 1, stride=1, stride_axis=0)
        high, low = split(moved)
        high, low = high.astype(F32), low.astype(F32)
        high = high + pltpu.roll(high, 64, 1)
        low = low + pltpu.roll(low, 64, 1)
        table_ref[b * rows : (b + 1) * rows, :LW] = high.astype(BF)
        table_ref[b * rows : (b + 1) * rows, LW:] = low.astype(BF)


def build_col_tables(taps_ref, pad_ref, table_ref):
    pad_ref[...] = jnp.zeros_like(pad_ref)
    pad_ref[:NB, :KS] = taps_ref[...]
    lane, sub = iota((LW, LW), 1), iota((LW, LW), 0)
    for b in range(NB):
        wide = jnp.broadcast_to(pad_ref[b : b + 1, :], (LW, LW))
        moved = pltpu.roll(wide, 0, 1, stride=1, stride_axis=0)
        near = jnp.where(lane >= sub, moved, 0.0).T
        far = jnp.where(lane < sub, moved, 0.0).T
        for part, at in ((near, 0), (far, LW)):
            high, low = split(part)
            table_ref[b, at : at + LW, :LW] = high
            table_ref[b, at : at + LW, LW:] = low


def row_stage(frame_ref, row_table_ref, win_hi_ref, win_lo_ref, chunk, rows, cols):
    width = 256 if chunk * 256 < cols else LW
    start = chunk * 256
    lane = iota((64, LW), 1)
    pieces = []
    for at in range(start, start + width, LW):
        here = pltpu.roll(frame_ref[:, at : at + LW], KH, 1) if at < cols else jnp.zeros((64, LW), F32)
        prev = pltpu.roll(frame_ref[:, at - LW : at], KH, 1) if at > 0 else jnp.zeros((64, LW), F32)
        pieces.append(jnp.where(lane < KH, prev, here))
    moved = jnp.concatenate(pieces, axis=1) if len(pieces) > 1 else pieces[0]
    high, low = split(moved)
    stacked = jnp.concatenate([high, low, high, low], axis=0)
    blocks = cols // LW
    first = start // LW
    for b in range(NB):
        out = jnp.dot(row_table_ref[b * rows : (b + 1) * rows, :], stacked, preferred_element_type=F32)
        hi, lo = split(out)
        for ref, val in ((win_hi_ref, hi), (win_lo_ref, lo)):
            for i in range(width // LW):
                part = val[:, i * LW : (i + 1) * LW]
                k = first + i
                if k < blocks:
                    ref[b, k, :, :LW] = part
                if k > 0:
                    ref[b, k - 1, :, LW:] = part


def col_stage(win_hi_ref, win_lo_ref, col_table_ref, resp_ref, rows, cols):
    blocks = cols // LW
    per = 8

    def body(b, carry):
        table = col_table_ref[b]
        for k in range(0, blocks, per):
            hi = win_hi_ref[b, k : k + per].reshape(per * rows, 2 * LW)
            lo = win_lo_ref[b, k : k + per].reshape(per * rows, 2 * LW)
            out = jnp.dot(hi, table, preferred_element_type=F32) + jnp.dot(lo, table, preferred_element_type=F32)
            resp_ref[b, k : k + per] = (out[:, :LW] + out[:, LW:]).reshape(per, rows, LW)
        return carry

    lax.fori_loop(0, NB, body, 0)


def pack_stamps(resp_ref, rows_ref, cols_ref, left_ref, right_ref, first_row, rows, cols, stamps):
    groups = rows // 8
    lane3 = iota((1, 1, LW), 2)
    lane2 = iota((8, LW), 1)

    def body(q, carry):
        packed = None
        rowv = jnp.full((8, LW), -(1 << 20), jnp.int32)
        colv = jnp.zeros((8, LW), jnp.int32)
        for t in range(3):
            s = q * 3 + t
            held = jnp.minimum(s, stamps - 1)
            left = jnp.clip(cols_ref[0, held] - HS, 0, cols - 1)
            row = jnp.where(s < stamps, rows_ref[0, held], -(1 << 20))
            k = left // LW
            off = left - k * LW
            near, far = resp_ref[:, k], resp_ref[:, k + 1]
            both = jnp.where(lane3 >= off, near, far)
            shift = lax.rem(SLOT * t - off + LW, LW)
            flat = pltpu.roll(both.reshape(SCI_PLANE + 1 - 0, rows, LW).reshape(-1, LW), shift, 1)
            flat = flat.reshape(SCI_PLANE + 1, rows, LW)
            packed = flat if packed is None else jnp.where(lane3 >= SLOT * t, flat, packed)
            inside = (lane2 >= SLOT * t) & (lane2 < SLOT * t + 2 * HS + 1)
            rowv = jnp.where(inside, row, rowv)
            colv = jnp.where(inside, left + lane2 - SLOT * t, colv)
        xv = colv.astype(F32) * (2.0 / cols) - 1.0
        at = pl.multiple_of(q * LW, LW)
        tail = jnp.zeros((PLANES - SCI_PLANE - 1, 8, LW), F32)
        for g in range(groups):
            yv = first_row + 8 * g + iota((8, LW), 0)
            hit = (jnp.abs(yv - rowv) <= HS).astype(F32)
            planes = jnp.concatenate([packed[:, 8 * g : 8 * g + 8, :], tail], axis=0)
            high, low = split(planes.reshape(PLANES * 8, LW))
            right_ref[g, : PLANES * 8, pl.ds(at, LW)] = high
            right_ref[g, PLANES * 8 :, pl.ds(at, LW)] = low
            moment = planes * hit[None]
            for m in range(3):
                if m:
                    moment = moment * xv[None]
                high, low = split(moment.reshape(PLANES * 8, LW))
                left_ref[g, m * PLANES * 8 : (m + 1) * PLANES * 8, pl.ds(at, LW)] = high
                left_ref[g, (m + 3) * PLANES * 8 : (m + 4) * PLANES * 8, pl.ds(at, LW)] = low
        return carry

    lax.fori_loop(0, (stamps + 2) // 3, body, 0)


def normal_part(left_ref, right_ref, first_row, rows, total_rows):
    groups = rows // 8
    span = PLANES * 8
    same_y = (lax.rem(iota((8, span), 1), 8) == iota((8, span), 0)).astype(F32)
    plane, col = iota((span, LW), 0) // 8, iota((span, LW), 1)
    kind, base = col // 16, lax.rem(col, 16)
    match = plane == base
    real = match & (plane < NB)
    total = None
    for g in range(groups):
        out = lax.dot_general(left_ref[g], right_ref[g], (((1,), (1,)), ((), ())), preferred_element_type=F32)
        folded = out[: 3 * span, :span] + out[: 3 * span, span:] + out[3 * span :, :span]
        picked = jnp.sum(folded.reshape(3 * PLANES, 8, span) * same_y[None], axis=1)
        y = (2.0 / total_rows) * (first_row + 8 * g + lax.rem(iota((span, LW), 0), 8)).astype(F32) - 1.0
        zero = jnp.zeros((span, LW), F32)
        plain = jnp.where(match & (kind == 0), 1.0, zero)
        in_x = jnp.where(real & (kind == 1), 1.0, zero)
        in_y = jnp.where(real & (kind == 2), y, zero)
        maps = jnp.concatenate([plain + in_y, in_x, (plain + in_y) * y, in_x * y], axis=1)
        part = jnp.dot(picked, maps, precision=HIGHEST_MODE, preferred_element_type=F32)
        total = part if total is None else total + part
    return jnp.concatenate(
        [
            total[0:16, 0:LW] + total[16:32, LW : 2 * LW],
            total[16:32, 0:LW] + total[32:48, LW : 2 * LW],
            total[0:16, 2 * LW : 3 * LW] + total[16:32, 3 * LW :],
        ],
        axis=0,
    )


PIVOTS = [*range(0, 13), *range(16, 28), *range(32, 44)]


def solve(normal):
    sub, lane = iota((48, LW), 0), iota((48, LW), 1)
    live = (lax.rem(sub, 16) < NB) | (sub == ONE_PLANE)
    mat = jnp.where((sub == lane) & live, normal + RIDGE_WEIGHT, normal)
    for k in PIVOTS:
        column = jnp.broadcast_to(mat[:, k : k + 1], (48, LW))
        pivot = column[k : k + 1, :]
        row = mat[k : k + 1, :] / pivot
        mat = jnp.where(sub == k, row, mat - column * row)
    return mat[:, SCI_PLANE : SCI_PLANE + 1]


def coeff_row(answer):
    sub, lane = iota((48, LW), 0), iota((48, LW), 1)
    kind, base = sub // 16, lax.rem(sub, 16)
    goes = jnp.where(base < NB, kind * NB + base, jnp.where(sub == ONE_PLANE, NU - 1, -1))
    return jnp.sum(jnp.where(goes == lane, answer, 0.0), axis=0, keepdims=True)


def apply_model(answer, resp_ref, out_ref, first_row, rows, total_rows, cols):
    wide = jnp.broadcast_to(answer, (48, LW))
    lift = lambda i: jnp.broadcast_to(wide[i : i + 1, :], (8, LW))
    blocks = cols // LW
    const = lift(ONE_PLANE)
    for g in range(rows // 8):
        y = (2.0 / total_rows) * (first_row + 8 * g + iota((8, LW), 0)).astype(F32) - 1.0
        level = [lift(b) + y * lift(32 + b) for b in range(NB)]
        slope = [lift(16 + b) for b in range(NB)]

        def body(k, carry):
            flat = const
            tilt = jnp.zeros((8, LW), F32)
            for b in range(NB):
                r = resp_ref[b, k, 8 * g : 8 * g + 8, :]
                flat = flat + level[b] * r
                tilt = tilt + slope[b] * r
            at = pl.multiple_of(k * LW, LW)
            x = (k * LW + iota((8, LW), 1)).astype(F32) * (2.0 / cols) - 1.0
            out_ref[0, 8 * g : 8 * g + 8, pl.ds(at, LW)] = resp_ref[SCI_PLANE, k, 8 * g : 8 * g + 8, :] - (flat + x * tilt)
            return carry

        lax.fori_loop(0, blocks, body, 0, unroll=4)


def kernel(
    dets, strips,
    sci_ref, tmpl_ref, row_ref, col_ref, srow_ref, scol_ref,
    out_ref, coef_ref,
    frame, pad, row_table, col_table, win_hi, win_lo, resp, left, right, parts, sci_buf,
    main_send, main_recv, up_send, up_recv, down_send, down_recv, part_send, part_recv, own_sem, sci_sem,
):
    _, rows, cols = sci_ref.shape
    width = tmpl_ref.shape[2]
    total_rows = rows * strips
    det, strip = lax.axis_index("det"), lax.axis_index("strip")
    above, below = strip > 0, strip < strips - 1
    first_row = strip * rows

    frame[0:HALO, :] = jnp.zeros((HALO, cols), F32)
    frame[HALO + rows :, :] = jnp.zeros((HALO, cols), F32)

    barrier = pltpu.get_barrier_semaphore()

    def greet(target_det, target_strip):
        pl.semaphore_signal(barrier, inc=1, device_id=(target_det, target_strip), device_id_type=MESH)

    for i in range(1, dets):
        greet(lax.rem(det + i, dets), strip)

    @pl.when(above)
    def _():
        for i in range(dets):
            greet(lax.rem(det + i, dets), strip - 1)

    @pl.when(below)
    def _():
        for i in range(dets):
            greet(lax.rem(det + i, dets), strip + 1)

    for i in range(2, strips - 1):
        other = lax.rem(strip + i, strips)

        @pl.when((other != strip - 1) & (other != strip + 1))
        def _():
            greet(det, other)

    @pl.when(strip == 0)
    def _():
        greet(det, strips - 1)

    @pl.when(strip == strips - 1)
    def _():
        greet(det, 0)

    ends = jnp.where(above & below, 0, 1)
    count = (dets - 1) + dets * (2 - ends) + (strips - 3 + ends)
    pl.semaphore_wait(barrier, count)

    def main_copy(i):
        target = lax.rem(det + i, dets)
        return pltpu.make_async_remote_copy(
            tmpl_ref.at[target], frame.at[pl.ds(HALO, rows), pl.ds(pl.multiple_of(det * width, width), width)],
            main_send.at[i], main_recv.at[i], device_id=(target, strip), device_id_type=MESH,
        )

    def up_copy(i):
        target = lax.rem(det + i, dets)
        return pltpu.make_async_remote_copy(
            tmpl_ref.at[target, pl.ds(0, HALO), :],
            frame.at[pl.ds(HALO + rows, HALO), pl.ds(pl.multiple_of(det * width, width), width)],
            up_send.at[i], up_recv.at[i], device_id=(target, strip - 1), device_id_type=MESH,
        )

    def down_copy(i):
        target = lax.rem(det + i, dets)
        return pltpu.make_async_remote_copy(
            tmpl_ref.at[target, pl.ds(rows - HALO, HALO), :],
            frame.at[pl.ds(0, HALO), pl.ds(pl.multiple_of(det * width, width), width)],
            down_send.at[i], down_recv.at[i], device_id=(target, strip + 1), device_id_type=MESH,
        )

    own = pltpu.make_async_copy(
        tmpl_ref.at[det], frame.at[pl.ds(HALO, rows), pl.ds(pl.multiple_of(det * width, width), width)], own_sem
    )
    own.start()
    sci_copy = pltpu.make_async_copy(sci_ref.at[0], sci_buf, sci_sem)
    sci_copy.start()
    for i in range(dets):
        if i:
            main_copy(i).start()

        @pl.when(above)
        def _():
            up_copy(i).start()

        @pl.when(below)
        def _():
            down_copy(i).start()

    build_row_table(row_ref, pad, row_table, rows)
    build_col_tables(col_ref, pad, col_table)
    blocks = cols // LW
    sci_copy.wait()
    for k in range(blocks):
        resp[SCI_PLANE, k] = sci_buf[:, k * LW : (k + 1) * LW]
    resp[ONE_PLANE] = jnp.ones((blocks + 1, rows, LW), F32)
    resp[:ONE_PLANE, blocks] = jnp.zeros((NB, rows, LW), F32)
    resp[SCI_PLANE, blocks] = jnp.zeros((rows, LW), F32)

    own.wait()
    for i in range(dets):
        if i:
            main_copy(i).wait()

        @pl.when(above)
        def _():
            up_copy(i).wait_send()
            down_copy(i).wait_recv()

        @pl.when(below)
        def _():
            down_copy(i).wait_send()
            up_copy(i).wait_recv()

    for chunk in range(cols // 256 + 1):
        row_stage(frame, row_table, win_hi, win_lo, chunk, rows, cols)
    col_stage(win_hi, win_lo, col_table, resp, rows, cols)
    pack_stamps(resp, srow_ref, scol_ref, left, right, first_row, rows, cols, srow_ref.shape[1])
    parts[strip] = normal_part(left, right, first_row, rows, total_rows)

    def part_copy(i):
        return pltpu.make_async_remote_copy(
            parts.at[strip], parts.at[strip], part_send.at[i], part_recv.at[i],
            device_id=(det, lax.rem(strip + i, strips)), device_id_type=MESH,
        )

    for i in range(1, strips):
        part_copy(i).start()
    for i in range(1, strips):
        source = lax.rem(strip + strips - i, strips)
        part_copy(i).wait_send()
        pltpu.make_async_remote_copy(
            parts.at[source], parts.at[source], part_send.at[i], part_recv.at[i],
            device_id=(det, source), device_id_type=MESH,
        ).wait_recv()
    normal = parts[0]
    for i in range(1, strips):
        normal = normal + parts[i]
    answer = solve(normal)
    coef_ref[...] = coeff_row(answer)[:, :NU]
    apply_model(answer, resp, out_ref, first_row, rows, total_rows, cols)


def local(dets, strips, science, template, row_taps, col_taps, stamp_rows, stamp_cols):
    _, rows, cols = science.shape
    blocks = cols // LW
    stamps = stamp_rows.shape[1]
    packed = (stamps + 2) // 3 * LW
    any_space = pl.BlockSpec(memory_space=pl.ANY)
    vmem = pl.BlockSpec(memory_space=pltpu.VMEM)
    smem = pl.BlockSpec(memory_space=pltpu.SMEM)
    dma = pltpu.SemaphoreType.DMA
    return pl.pallas_call(
        functools.partial(kernel, dets, strips),
        out_shape=(jax.ShapeDtypeStruct(science.shape, F32), jax.ShapeDtypeStruct((1, NU), F32)),
        in_specs=[any_space, any_space, vmem, vmem, smem, smem],
        out_specs=(vmem, vmem),
        scratch_shapes=[
            pltpu.VMEM((rows + 2 * HALO, cols), F32),
            pltpu.VMEM((16, LW), F32),
            pltpu.VMEM((NB * rows, 256), BF),
            pltpu.VMEM((NB, 256, 256), BF),
            pltpu.VMEM((NB, blocks, rows, 256), BF),
            pltpu.VMEM((NB, blocks, rows, 256), BF),
            pltpu.VMEM((SCI_PLANE + 1, blocks + 1, rows, LW), F32),
            pltpu.VMEM((rows // 8, 6 * PLANES * 8, packed), BF),
            pltpu.VMEM((rows // 8, 2 * PLANES * 8, packed), BF),
            pltpu.VMEM((strips, 48, LW), F32),
            pltpu.VMEM((rows, cols), F32),
            dma((dets,)), dma((dets,)), dma((dets,)), dma((dets,)), dma((dets,)), dma((dets,)),
            dma((strips,)), dma((strips,)), dma, dma,
        ],
        compiler_params=pltpu.CompilerParams(
            collective_id=0, has_side_effects=True, vmem_limit_bytes=56 * 1024 * 1024
        ),
    )(science, template, row_taps, col_taps, stamp_rows, stamp_cols)


def solution(mesh):
    return jax.shard_map(
        functools.partial(local, mesh.shape["det"], mesh.shape["strip"]),
        mesh=mesh,
        in_specs=(
            P("det", "strip", None),
            P(None, "strip", "det"),
            P(),
            P(),
            P("det", None),
            P("det", None),
        ),
        out_specs=(P("det", "strip", None), P("det", None)),
        check_vma=False,
    )
```

time: 234 us -> 59.7 us (0.26)
  the two profiles are of different devices: /device:TPU:0 before, /device:TPU:1 now
where the time goes in v1:
time: 59.7 us; the launch traced here: 59.5 us
  Pallas kernels  56.5 us (95%)
  local copies, waits for them, and re-layouts  2.38 us (4%)
  between operations  0.65 us (1%)
    pallas_call x1, Pallas kernels, local(): pl.pallas_call(functools.partial(kernel, dets, strips), out_shape=(jax.Sh...  56.5 us
    unnamed x4, local copies, waits for them, and re-layouts  2.38 us

profile of v1, /device:TPU:1, one launch (start us, length us, event | category | flops | bytes accessed | tf_op | source)
XLA Modules:
  0.0 59.5 jit_solution(18140243798233094023)
XLA Ops:
  0.6 56.5 %shard_map.77 = (f32[1,32,4096]{2,1,0:T(8,128)}, f32[1,37]{1,0:T(1,128)}) custom-call(f32[1,32,4096]{2,1,0:T(8,128)} %sci_ref.1, f32[16,32,256]{2,1,0:T(8,128)} %tmpl_ref.1, f32[12,21]{1,0:T(8,128)} %row_ref.1, f32[12,21]{1,0:T(8,128)} %col_ref.1, s32[1,32]{1,0:T(1,128)} %srow_ref.1, s32[1,32]{1,0:T(1,128)} %scol_ref.1), custom_call_target="tpu_custom_call" | custom-call | tf_op jit(solution)/shard_map/pallas_call | solution.py:392
  57.1 0.0 copy-start
  57.1 1.9 %copy.10 = f32[1,32,4096]{2,1,0:T(8,128)} copy(f32[1,32,4096]{2,1,0:T(8,128)} %get-tuple-element.4) | data formatting | bytes 1048576
  59.0 0.0 copy-done
  59.0 0.5 copy.11
Async XLA Ops:
  57.1 1.9 %copy-start = (f32[1,37]{1,0:T(1,128)S(1)}, f32[1,37]{1,0:T(1,128)}, u32[]{:S(2)}) copy-start(f32[1,37]{1,0:T(1,128)} %get-tuple-element.5) | copy-start | bytes 448

commit v2 on v1

--- a/solution.py
+++ b/solution.py
@@ -63,7 +63,7 @@
             table_ref[b, at : at + LW, LW:] = low
 
 
-def row_stage(frame_ref, row_table_ref, win_hi_ref, win_lo_ref, chunk, rows, cols):
+def row_stage(frame_ref, row_table_ref, win_hi_ref, win_lo_ref, chunk, first_row, rows, cols, total_rows):
     width = 256 if chunk * 256 < cols else LW
     start = chunk * 256
     lane = iota((64, LW), 1)
@@ -73,6 +73,10 @@
         prev = pltpu.roll(frame_ref[:, at - LW : at], KH, 1) if at > 0 else jnp.zeros((64, LW), F32)
         pieces.append(jnp.where(lane < KH, prev, here))
     moved = jnp.concatenate(pieces, axis=1) if len(pieces) > 1 else pieces[0]
+    sub = iota(moved.shape, 0)
+    sky = first_row - HALO + sub
+    held = (sub >= HALO - KH) & (sub < HALO + rows + KH) & (sky >= 0) & (sky < total_rows)
+    moved = jnp.where(held, moved, 0.0)
     high, low = split(moved)
     stacked = jnp.concatenate([high, low, high, low], axis=0)
     blocks = cols // LW
@@ -245,46 +249,6 @@
     above, below = strip > 0, strip < strips - 1
     first_row = strip * rows
 
-    frame[0:HALO, :] = jnp.zeros((HALO, cols), F32)
-    frame[HALO + rows :, :] = jnp.zeros((HALO, cols), F32)
-
-    barrier = pltpu.get_barrier_semaphore()
-
-    def greet(target_det, target_strip):
-        pl.semaphore_signal(barrier, inc=1, device_id=(target_det, target_strip), device_id_type=MESH)
-
-    for i in range(1, dets):
-        greet(lax.rem(det + i, dets), strip)
-
-    @pl.when(above)
-    def _():
-        for i in range(dets):
-            greet(lax.rem(det + i, dets), strip - 1)
-
-    @pl.when(below)
-    def _():
-        for i in range(dets):
-            greet(lax.rem(det + i, dets), strip + 1)
-
-    for i in range(2, strips - 1):
-        other = lax.rem(strip + i, strips)
-
-        @pl.when((other != strip - 1) & (other != strip + 1))
-        def _():
-            greet(det, other)
-
-    @pl.when(strip == 0)
-    def _():
-        greet(det, strips - 1)
-
-    @pl.when(strip == strips - 1)
-    def _():
-        greet(det, 0)
-
-    ends = jnp.where(above & below, 0, 1)
-    count = (dets - 1) + dets * (2 - ends) + (strips - 3 + ends)
-    pl.semaphore_wait(barrier, count)
-
     def main_copy(i):
         target = lax.rem(det + i, dets)
         return pltpu.make_async_remote_copy(
@@ -292,20 +256,24 @@
             main_send.at[i], main_recv.at[i], device_id=(target, strip), device_id_type=MESH,
         )
 
-    def up_copy(i):
+    here = pl.ds(pl.multiple_of(det * width, width), width)
+    ups = ((0, 8), (8, KH - 8))
+    downs = ((rows - 8, 8), (rows - KH, KH - 8))
+
+    def up_copy(i, p):
         target = lax.rem(det + i, dets)
+        at, size = ups[p]
         return pltpu.make_async_remote_copy(
-            tmpl_ref.at[target, pl.ds(0, HALO), :],
-            frame.at[pl.ds(HALO + rows, HALO), pl.ds(pl.multiple_of(det * width, width), width)],
-            up_send.at[i], up_recv.at[i], device_id=(target, strip - 1), device_id_type=MESH,
+            tmpl_ref.at[target, pl.ds(at, size), :], frame.at[pl.ds(HALO + rows + at, size), here],
+            up_send.at[p, i], up_recv.at[p, i], device_id=(target, strip - 1), device_id_type=MESH,
         )
 
-    def down_copy(i):
+    def down_copy(i, p):
         target = lax.rem(det + i, dets)
+        at, size = downs[p]
         return pltpu.make_async_remote_copy(
-            tmpl_ref.at[target, pl.ds(rows - HALO, HALO), :],
-            frame.at[pl.ds(0, HALO), pl.ds(pl.multiple_of(det * width, width), width)],
-            down_send.at[i], down_recv.at[i], device_id=(target, strip + 1), device_id_type=MESH,
+            tmpl_ref.at[target, pl.ds(at, size), :], frame.at[pl.ds(HALO - rows + at, size), here],
+            down_send.at[p, i], down_recv.at[p, i], device_id=(target, strip + 1), device_id_type=MESH,
         )
 
     own = pltpu.make_async_copy(
@@ -320,11 +288,13 @@
 
         @pl.when(above)
         def _():
-            up_copy(i).start()
+            up_copy(i, 0).start()
+            up_copy(i, 1).start()
 
         @pl.when(below)
         def _():
-            down_copy(i).start()
+            down_copy(i, 0).start()
+            down_copy(i, 1).start()
 
     build_row_table(row_ref, pad, row_table, rows)
     build_col_tables(col_ref, pad, col_table)
@@ -343,16 +313,18 @@
 
         @pl.when(above)
         def _():
-            up_copy(i).wait_send()
-            down_copy(i).wait_recv()
+            for p in range(2):
+                up_copy(i, p).wait_send()
+                down_copy(i, p).wait_recv()
 
         @pl.when(below)
         def _():
-            down_copy(i).wait_send()
-            up_copy(i).wait_recv()
+            for p in range(2):
+                down_copy(i, p).wait_send()
+                up_copy(i, p).wait_recv()
 
     for chunk in range(cols // 256 + 1):
-        row_stage(frame, row_table, win_hi, win_lo, chunk, rows, cols)
+        row_stage(frame, row_table, win_hi, win_lo, chunk, first_row, rows, cols, total_rows)
     col_stage(win_hi, win_lo, col_table, resp, rows, cols)
     pack_stamps(resp, srow_ref, scol_ref, left, right, first_row, rows, cols, srow_ref.shape[1])
     parts[strip] = normal_part(left, right, first_row, rows, total_rows)
@@ -406,11 +378,11 @@
             pltpu.VMEM((rows // 8, 2 * PLANES * 8, packed), BF),
             pltpu.VMEM((strips, 48, LW), F32),
             pltpu.VMEM((rows, cols), F32),
-            dma((dets,)), dma((dets,)), dma((dets,)), dma((dets,)), dma((dets,)), dma((dets,)),
+            dma((dets,)), dma((dets,)), dma((2, dets)), dma((2, dets)), dma((2, dets)), dma((2, dets)),
             dma((strips,)), dma((strips,)), dma, dma,
         ],
         compiler_params=pltpu.CompilerParams(
-            collective_id=0, has_side_effects=True, vmem_limit_bytes=56 * 1024 * 1024
+            has_side_effects=True, vmem_limit_bytes=56 * 1024 * 1024
         ),
     )(science, template, row_taps, col_taps, stamp_rows, stamp_cols)
 

time: 59.7 us -> 62.3 us (1.044)
  the two profiles are of different devices: /device:TPU:1 before, /device:TPU:0 now
where the time goes in v2:
time: 62.3 us; the launch traced here: 61.5 us
  Pallas kernels  58.5 us (94%)
  local copies, waits for them, and re-layouts  2.38 us (4%)
  between operations  0.65 us (1%)
    pallas_call x1, Pallas kernels, local(): pl.pallas_call(functools.partial(kernel, dets, strips), out_shape=(jax.Sh...  58.5 us
    unnamed x4, local copies, waits for them, and re-layouts  2.38 us

profile of v2, /device:TPU:0, one launch (start us, length us, event | category | flops | bytes accessed | tf_op | source)
XLA Modules:
  0.0 61.5 jit_solution(7930093063508804587)
XLA Ops:
  0.6 58.5 %shard_map.77 = (f32[1,32,4096]{2,1,0:T(8,128)}, f32[1,37]{1,0:T(1,128)}) custom-call(f32[1,32,4096]{2,1,0:T(8,128)} %sci_ref.1, f32[16,32,256]{2,1,0:T(8,128)} %tmpl_ref.1, f32[12,21]{1,0:T(8,128)} %row_ref.1, f32[12,21]{1,0:T(8,128)} %col_ref.1, s32[1,32]{1,0:T(1,128)} %srow_ref.1, s32[1,32]{1,0:T(1,128)} %scol_ref.1), custom_call_target="tpu_custom_call" | custom-call | tf_op jit(solution)/shard_map/pallas_call | solution.py:364
  59.1 0.0 copy-start
  59.2 1.9 %copy.10 = f32[1,32,4096]{2,1,0:T(8,128)} copy(f32[1,32,4096]{2,1,0:T(8,128)} %get-tuple-element.4) | data formatting | bytes 1048576
  61.0 0.0 copy-done
  61.0 0.5 copy.11
Async XLA Ops:
  59.1 1.9 %copy-start = (f32[1,37]{1,0:T(1,128)S(1)}, f32[1,37]{1,0:T(1,128)}, u32[]{:S(2)}) copy-start(f32[1,37]{1,0:T(1,128)} %get-tuple-element.5) | copy-start | bytes 448

commit v3 on v2

v3 whole, which is shorter than its diff:
```python
import functools

import jax
import jax.numpy as jnp
from jax import lax
from jax.experimental import pallas as pl
from jax.experimental.pallas import tpu as pltpu
from jax.sharding import PartitionSpec as P

NB = 12
KS = 21
HS = 17
KH = 10
NU = 37
LW = 128
HALO = 16
SLOT = 64
PLANES = 16
ONE_PLANE = 12
SCI_PLANE = 13
RIDGE_WEIGHT = 1.0
HIGHEST_MODE = lax.Precision.HIGHEST
MESH = pl.DeviceIdType.MESH
BF = jnp.bfloat16
F32 = jnp.float32


def iota(shape, dim):
    return lax.broadcasted_iota(jnp.int32, shape, dim)


def split(value):
    high = value.astype(BF)
    return high, (value - high.astype(F32)).astype(BF)


def build_row_table(taps_ref, pad_ref, table_ref, rows):
    pad_ref[...] = jnp.zeros_like(pad_ref)
    pad_ref[:NB, :KS] = taps_ref[...]
    for b in range(NB):
        wide = jnp.broadcast_to(pad_ref[b : b + 1, :], (rows, LW))
        moved = pltpu.roll(wide, HALO - KH, 1, stride=1, stride_axis=0)
        high, low = split(moved)
        high, low = high.astype(F32), low.astype(F32)
        high = high + pltpu.roll(high, 64, 1)
        low = low + pltpu.roll(low, 64, 1)
        table_ref[b * rows : (b + 1) * rows, :LW] = high.astype(BF)
        table_ref[b * rows : (b + 1) * rows, LW:] = low.astype(BF)


def build_col_tables(taps_ref, pad_ref, table_ref, stamp_table_ref):
    pad_ref[...] = jnp.zeros_like(pad_ref)
    pad_ref[:NB, :KS] = taps_ref[...]
    lane, sub = iota((LW, LW), 1), iota((LW, LW), 0)
    same_slot = lane // SLOT == sub // SLOT
    for b in range(NB):
        wide = jnp.broadcast_to(pad_ref[b : b + 1, :], (LW, LW))
        moved = pltpu.roll(wide, 0, 1, stride=1, stride_axis=0)
        near = jnp.where(lane >= sub, moved, 0.0).T
        far = jnp.where(lane < sub, moved, 0.0).T
        for part, at in ((near, 0), (far, LW)):
            high, low = split(part)
            table_ref[b, at : at + LW, :LW] = high
            table_ref[b, at : at + LW, LW:] = low
        high, low = split(jnp.where(same_slot, near, 0.0))
        for at in (0, LW):
            stamp_table_ref[b, at : at + LW, :LW] = high
            stamp_table_ref[b, at : at + LW, LW:] = low


def row_filtered(row_table_ref, moved, rows):
    high, low = split(moved)
    stacked = jnp.concatenate([high, low, high, low], axis=0)
    size = NB // 2
    for base in (0, size):
        out = jnp.dot(row_table_ref[base * rows : (base + size) * rows, :], stacked, preferred_element_type=F32)
        yield base, [v.reshape(size, rows, moved.shape[1]) for v in split(out)]


def held_rows(width, first_row, rows, total_rows):
    sub = iota((2 * HALO + rows, width), 0)
    sky = first_row - HALO + sub
    return (sub >= HALO - KH) & (sub < HALO + rows + KH) & (sky >= 0) & (sky < total_rows)


def row_stage(sky_ref, row_table_ref, windows, first, count, rows):
    size = NB // 2
    lane = iota((2 * HALO + rows, LW), 1)
    loaded = [pltpu.roll(sky_ref[first + i], KH, 1) for i in range(count + 1)]
    moved = [jnp.where(lane < KH, loaded[i], loaded[i + 1]) for i in range(count)]
    moved = jnp.concatenate(moved, axis=1) if count > 1 else moved[0]
    for base, pair in row_filtered(row_table_ref, moved, rows):
        for ref, val in zip(windows, pair):
            for i in range(count):
                part = val[:, :, i * LW : (i + 1) * LW]
                ref[base : base + size, first + i + 1, :, :LW] = part
                ref[base : base + size, first + i, :, LW:] = part


def col_stage(windows, col_table_ref, resp_ref, rows, cols):
    blocks = cols // LW
    per = 8

    def body(b, carry):
        table = col_table_ref[b]
        for k in range(0, blocks, per):
            hi, lo = [ref[b, k + 1 : k + 1 + per].reshape(per * rows, 2 * LW) for ref in windows]
            out = jnp.dot(hi, table, preferred_element_type=F32) + jnp.dot(lo, table, preferred_element_type=F32)
            resp_ref[b, k : k + per] = (out[:, :LW] + out[:, LW:]).reshape(per, rows, LW)
        return carry

    lax.fori_loop(0, NB, body, 0)


def gather(ref, starts):
    picked = []
    for t, start in enumerate(starts):
        k = start // LW
        off = start - k * LW
        near, far = ref[k], ref[k + 1]
        both = jnp.where(iota(near.shape, 1) >= off, near, far)
        picked.append(pltpu.roll(both, lax.rem(SLOT * t - off + LW, LW), 1))
    return jnp.where(iota(picked[0].shape, 1) < SLOT, *picked)


def stamp_left(cols_ref, s, cols):
    return jnp.clip(cols_ref[0, s] - HS, 0, cols - 1)


def stamp_responses(sky_ref, row_table_ref, stamp_table_ref, win_ref, resp_ref, cols_ref, rows, cols):
    pairs = resp_ref.shape[1]
    size = NB // 2

    def body(u, carry):
        lefts = [stamp_left(cols_ref, 4 * u + t, cols) + (LW - KH) for t in range(4)]
        moved = jnp.concatenate([gather(sky_ref, lefts[:2]), gather(sky_ref, lefts[2:])], axis=1)
        for base, pair in row_filtered(row_table_ref, moved, rows):
            for part, val in enumerate(pair):
                for i in range(2):
                    win_ref[base : base + size, 2 * u + i, :, part * LW : (part + 1) * LW] = val[:, :, i * LW : (i + 1) * LW]
        return carry

    lax.fori_loop(0, pairs // 2, body, 0)

    def filt(b, carry):
        out = jnp.dot(win_ref[b].reshape(pairs * rows, 2 * LW), stamp_table_ref[b], preferred_element_type=F32)
        resp_ref[b] = (out[:, :LW] + out[:, LW:]).reshape(pairs, rows, LW)
        return carry

    lax.fori_loop(0, NB, filt, 0)


def pack_stamps(resp_ref, sci_ref, rows_ref, cols_ref, left_ref, right_ref, first_row, rows, cols):
    groups = rows // 8
    lane = iota((8, LW), 1)

    def body(q, carry):
        lefts = [stamp_left(cols_ref, 2 * q + t, cols) for t in range(2)]
        second = lane >= SLOT
        inside = lane - jnp.where(second, SLOT, 0)
        rowv = jnp.where(second, rows_ref[0, 2 * q + 1], rows_ref[0, 2 * q])
        xv = (jnp.where(second, lefts[1], lefts[0]) + inside).astype(F32) * (2.0 / cols) - 1.0
        sci = gather(sci_ref, lefts)
        at = pl.multiple_of(q * LW, LW)
        ones, zeros = jnp.ones((1, 8, LW), F32), jnp.zeros((PLANES - SCI_PLANE - 1, 8, LW), F32)
        for g in range(groups):
            near = slice(8 * g, 8 * g + 8)
            yv = first_row + 8 * g + iota((8, LW), 0)
            hit = ((jnp.abs(yv - rowv) <= HS) & (inside < 2 * HS + 1)).astype(F32)
            planes = jnp.concatenate([resp_ref[:, q, near, :], ones, sci[None, near, :], zeros], axis=0)
            high, low = split(planes.reshape(PLANES * 8, LW))
            right_ref[g, : PLANES * 8, pl.ds(at, LW)] = high
            right_ref[g, PLANES * 8 :, pl.ds(at, LW)] = low
            moment = planes * hit[None]
            for m in range(3):
                if m:
                    moment = moment * xv[None]
                high, low = split(moment.reshape(PLANES * 8, LW))
                left_ref[g, m * PLANES * 8 : (m + 1) * PLANES * 8, pl.ds(at, LW)] = high
                left_ref[g, (m + 3) * PLANES * 8 : (m + 4) * PLANES * 8, pl.ds(at, LW)] = low
        return carry

    lax.fori_loop(0, resp_ref.shape[1], body, 0)


def build_maps(maps_ref, first_row, rows, total_rows):
    span = PLANES * 8
    plane, col = iota((span, LW), 0) // 8, iota((span, LW), 1)
    kind, base = col // 16, lax.rem(col, 16)
    match = plane == base
    real = match & (plane < NB)
    zero = jnp.zeros((span, LW), F32)
    plain = jnp.where(match & (kind == 0), 1.0, zero)
    in_x = jnp.where(real & (kind == 1), 1.0, zero)
    for g in range(rows // 8):
        y = (2.0 / total_rows) * (first_row + 8 * g + lax.rem(iota((span, LW), 0), 8)).astype(F32) - 1.0
        level = plain + jnp.where(real & (kind == 2), y, zero)
        for i, part in enumerate((level, in_x, level * y, in_x * y)):
            maps_ref[g * span : (g + 1) * span, i * LW : (i + 1) * LW] = part


def normal_part(left_ref, right_ref, maps_ref, rows):
    span = PLANES * 8
    same_y = (lax.rem(iota((8, span), 1), 8) == iota((8, span), 0)).astype(F32)
    picked = []
    for g in range(rows // 8):
        out = lax.dot_general(left_ref[g], right_ref[g], (((1,), (1,)), ((), ())), preferred_element_type=F32)
        folded = out[: 3 * span, :span] + out[: 3 * span, span:] + out[3 * span :, :span]
        picked.append(jnp.sum(folded.reshape(3 * PLANES, 8, span) * same_y[None], axis=1))
    total = jnp.dot(
        jnp.concatenate(picked, axis=1), maps_ref[...], precision=HIGHEST_MODE, preferred_element_type=F32
    )
    return jnp.concatenate(
        [
            total[0:16, 0:LW] + total[16:32, LW : 2 * LW],
            total[16:32, 0:LW] + total[32:48, LW : 2 * LW],
            total[0:16, 2 * LW : 3 * LW] + total[16:32, 3 * LW :],
        ],
        axis=0,
    )


PIVOTS = [*range(0, 13), *range(16, 28), *range(32, 44)]


def solve(normal):
    sub, lane = iota((48, LW), 0), iota((48, LW), 1)
    live = (lax.rem(sub, 16) < NB) | (sub == ONE_PLANE)
    mat = jnp.where((sub == lane) & live, normal + RIDGE_WEIGHT, normal)
    at = lambda value, k: value[k : k + 1, :]
    for i in range(0, NU - 1, 2):
        j, k = PIVOTS[i], PIVOTS[i + 1]
        cj = jnp.broadcast_to(mat[:, j : j + 1], (48, LW))
        ck = jnp.broadcast_to(mat[:, k : k + 1], (48, LW))
        jj, jk, kj, kk = at(cj, j), at(ck, j), at(cj, k), at(ck, k)
        scale = 1.0 / (jj * kk - jk * kj)
        rj, rk = at(mat, j), at(mat, k)
        nj = (kk * rj - jk * rk) * scale
        nk = (jj * rk - kj * rj) * scale
        mat = jnp.where(sub == j, nj, jnp.where(sub == k, nk, mat - cj * nj - ck * nk))
    k = PIVOTS[-1]
    column = jnp.broadcast_to(mat[:, k : k + 1], (48, LW))
    row = at(mat, k) / at(column, k)
    mat = jnp.where(sub == k, row, mat - column * row)
    return mat[:, SCI_PLANE : SCI_PLANE + 1]


def coeff_row(answer):
    sub, lane = iota((48, LW), 0), iota((48, LW), 1)
    kind, base = sub // 16, lax.rem(sub, 16)
    goes = jnp.where(base < NB, kind * NB + base, jnp.where(sub == ONE_PLANE, NU - 1, -1))
    return jnp.sum(jnp.where(goes == lane, answer, 0.0), axis=0, keepdims=True)


def apply_model(answer, resp_ref, sci_ref, out_ref, first_row, rows, total_rows, cols):
    wide = jnp.broadcast_to(answer, (48, LW))
    lift = lambda i: jnp.broadcast_to(wide[i : i + 1, :], (8, LW))
    blocks = cols // LW
    const = lift(ONE_PLANE)
    for g in range(rows // 8):
        y = (2.0 / total_rows) * (first_row + 8 * g + iota((8, LW), 0)).astype(F32) - 1.0
        level = [lift(b) + y * lift(32 + b) for b in range(NB)]
        slope = [lift(16 + b) for b in range(NB)]

        def body(k, carry):
            flat = const
            tilt = jnp.zeros((8, LW), F32)
            for b in range(NB):
                r = resp_ref[b, k, 8 * g : 8 * g + 8, :]
                flat = flat + level[b] * r
                tilt = tilt + slope[b] * r
            at = pl.multiple_of(k * LW, LW)
            x = (k * LW + iota((8, LW), 1)).astype(F32) * (2.0 / cols) - 1.0
            out_ref[0, 8 * g : 8 * g + 8, pl.ds(at, LW)] = sci_ref[k, 8 * g : 8 * g + 8, :] - (flat + x * tilt)
            return carry

        lax.fori_loop(0, blocks, body, 0, unroll=4)


def kernel(
    dets, strips,
    sci_ref, tmpl_ref, row_ref, col_ref, srow_ref, scol_ref,
    out_ref, coef_ref,
    frame, pad, row_table, col_table, stamp_table, win_hi, win_lo, resp, stamp_win, stamp_resp, left, right, maps, parts, sci_buf, sky, sci,
    main_send, main_recv, up_send, up_recv, down_send, down_recv, part_send, part_recv, own_sem, sci_sem,
):
    _, rows, cols = sci_ref.shape
    width = tmpl_ref.shape[2]
    total_rows = rows * strips
    det, strip = lax.axis_index("det"), lax.axis_index("strip")
    above, below = strip > 0, strip < strips - 1
    first_row = strip * rows

    barrier = pltpu.get_barrier_semaphore()

    def greet(target_det, target_strip):
        pl.semaphore_signal(barrier, inc=1, device_id=(target_det, target_strip), device_id_type=MESH)

    for i in range(1, dets):
        greet(lax.rem(det + i, dets), strip)

    @pl.when(above)
    def _():
        for i in range(dets):
            greet(lax.rem(det + i, dets), strip - 1)

    @pl.when(below)
    def _():
        for i in range(dets):
            greet(lax.rem(det + i, dets), strip + 1)

    for i in range(2, strips - 1):
        other = lax.rem(strip + i, strips)

        @pl.when((other != strip - 1) & (other != strip + 1))
        def _():
            greet(det, other)

    @pl.when(strip == 0)
    def _():
        greet(det, strips - 1)

    @pl.when(strip == strips - 1)
    def _():
        greet(det, 0)

    ends = jnp.where(above & below, 0, 1)
    count = (dets - 1) + dets * (2 - ends) + (strips - 3 + ends)
    pl.semaphore_wait(barrier, count)

    here = pl.ds(pl.multiple_of(det * width, width), width)

    def main_copy(i):
        target = lax.rem(det + dets - i, dets)
        return pltpu.make_async_remote_copy(
            tmpl_ref.at[target], frame.at[pl.ds(HALO, rows), here],
            main_send.at[i], main_recv.at[i], device_id=(target, strip), device_id_type=MESH,
        )

    ups = ((0, 8), (8, KH - 8))
    downs = ((rows - 8, 8), (rows - KH, KH - 8))

    def up_copy(i, p):
        target = lax.rem(det + dets - i, dets)
        at, size = ups[p]
        return pltpu.make_async_remote_copy(
            tmpl_ref.at[target, pl.ds(at, size), :], frame.at[pl.ds(HALO + rows + at, size), here],
            up_send.at[p, i], up_recv.at[p, i], device_id=(target, strip - 1), device_id_type=MESH,
        )

    def down_copy(i, p):
        target = lax.rem(det + dets - i, dets)
        at, size = downs[p]
        return pltpu.make_async_remote_copy(
            tmpl_ref.at[target, pl.ds(at, size), :], frame.at[pl.ds(HALO - rows + at, size), here],
            down_send.at[p, i], down_recv.at[p, i], device_id=(target, strip + 1), device_id_type=MESH,
        )

    own = pltpu.make_async_copy(
        tmpl_ref.at[det], frame.at[pl.ds(HALO, rows), here], own_sem
    )
    own.start()
    sci_copy = pltpu.make_async_copy(sci_ref.at[0], sci_buf, sci_sem)
    sci_copy.start()
    for i in range(dets):
        if i:
            main_copy(i).start()

        @pl.when(above)
        def _():
            up_copy(i, 0).start()
            up_copy(i, 1).start()

        @pl.when(below)
        def _():
            down_copy(i, 0).start()
            down_copy(i, 1).start()

    blocks = cols // LW
    sky[0] = jnp.zeros((2 * HALO + rows, LW), F32)
    sky[blocks + 1] = jnp.zeros((2 * HALO + rows, LW), F32)
    sci[blocks] = jnp.zeros((rows, LW), F32)
    build_row_table(row_ref, pad, row_table, rows)
    build_col_tables(col_ref, pad, col_table, stamp_table)
    build_maps(maps, first_row, rows, total_rows)
    sci_copy.wait()
    for k in range(blocks):
        sci[k] = sci_buf[:, k * LW : (k + 1) * LW]
    own.wait()
    for i in range(dets):
        if i:
            main_copy(i).wait_recv()

        @pl.when(above)
        def _():
            for p in range(2):
                down_copy(i, p).wait_recv()

        @pl.when(below)
        def _():
            for p in range(2):
                up_copy(i, p).wait_recv()

    held = held_rows(LW, first_row, rows, total_rows)
    for k in range(blocks):
        sky[k + 1] = jnp.where(held, frame[:, k * LW : (k + 1) * LW], 0.0)
    stamp_responses(sky, row_table, stamp_table, stamp_win, stamp_resp, scol_ref, rows, cols)
    pack_stamps(stamp_resp, sci, srow_ref, scol_ref, left, right, first_row, rows, cols)
    parts[strip] = normal_part(left, right, maps, rows)

    def part_copy(i):
        return pltpu.make_async_remote_copy(
            parts.at[strip], parts.at[strip], part_send.at[i], part_recv.at[i],
            device_id=(det, lax.rem(strip + i, strips)), device_id_type=MESH,
        )

    for i in range(1, strips):
        part_copy(i).start()
    windows = (win_hi, win_lo)

    def chunk(j, carry):
        row_stage(sky, row_table, windows, 2 * j, 2, rows)
        return carry

    lax.fori_loop(0, blocks // 2, chunk, 0)
    row_stage(sky, row_table, windows, blocks, 1, rows)
    col_stage(windows, col_table, resp, rows, cols)
    for i in range(1, strips):
        source = lax.rem(strip + strips - i, strips)
        part_copy(i).wait_send()
        pltpu.make_async_remote_copy(
            parts.at[source], parts.at[source], part_send.at[i], part_recv.at[i],
            device_id=(det, source), device_id_type=MESH,
        ).wait_recv()
    for i in range(dets):
        if i:
            main_copy(i).wait_send()

        @pl.when(above)
        def _():
            for p in range(2):
                up_copy(i, p).wait_send()

        @pl.when(below)
        def _():
            for p in range(2):
                down_copy(i, p).wait_send()

    normal = parts[0]
    for i in range(1, strips):
        normal = normal + parts[i]
    answer = solve(normal)
    coef_ref[...] = coeff_row(answer)[:, :NU]
    apply_model(answer, resp, sci, out_ref, first_row, rows, total_rows, cols)


def local(dets, strips, science, template, row_taps, col_taps, stamp_rows, stamp_cols):
    _, rows, cols = science.shape
    blocks = cols // LW
    stamps = stamp_rows.shape[1]
    packed = stamps // 2 * LW
    any_space = pl.BlockSpec(memory_space=pl.ANY)
    vmem = pl.BlockSpec(memory_space=pltpu.VMEM)
    smem = pl.BlockSpec(memory_space=pltpu.SMEM)
    dma = pltpu.SemaphoreType.DMA
    return pl.pallas_call(
        functools.partial(kernel, dets, strips),
        out_shape=(jax.ShapeDtypeStruct(science.shape, F32), jax.ShapeDtypeStruct((1, NU), F32)),
        in_specs=[any_space, any_space, vmem, vmem, smem, smem],
        out_specs=(vmem, vmem),
        scratch_shapes=[
            pltpu.VMEM((rows + 2 * HALO, cols), F32),
            pltpu.VMEM((16, LW), F32),
            pltpu.VMEM((NB * rows, 256), BF),
            pltpu.VMEM((NB, 256, 256), BF),
            pltpu.VMEM((NB, 256, 256), BF),
            pltpu.VMEM((NB, blocks + 2, rows, 256), BF),
            pltpu.VMEM((NB, blocks + 2, rows, 256), BF),
            pltpu.VMEM((NB, blocks, rows, LW), F32),
            pltpu.VMEM((NB, stamps // 2, rows, 256), BF),
            pltpu.VMEM((NB, stamps // 2, rows, LW), F32),
            pltpu.VMEM((rows // 8, 6 * PLANES * 8, packed), BF),
            pltpu.VMEM((rows // 8, 2 * PLANES * 8, packed), BF),
            pltpu.VMEM((rows * PLANES, 4 * LW), F32),
            pltpu.VMEM((strips, 48, LW), F32),
            pltpu.VMEM((rows, cols), F32),
            pltpu.VMEM((blocks + 2, rows + 2 * HALO, LW), F32),
            pltpu.VMEM((blocks + 1, rows, LW), F32),
            dma((dets,)), dma((dets,)), dma((2, dets)), dma((2, dets)), dma((2, dets)), dma((2, dets)),
            dma((strips,)), dma((strips,)), dma, dma,
        ],
        compiler_params=pltpu.CompilerParams(
            collective_id=0, has_side_effects=True, vmem_limit_bytes=56 * 1024 * 1024
        ),
    )(science, template, row_taps, col_taps, stamp_rows, stamp_cols)


def solution(mesh):
    return jax.shard_map(
        functools.partial(local, mesh.shape["det"], mesh.shape["strip"]),
        mesh=mesh,
        in_specs=(
            P("det", "strip", None),
            P(None, "strip", "det"),
            P(),
            P(),
            P("det", None),
            P("det", None),
        ),
        out_specs=(P("det", "strip", None), P("det", None)),
        check_vma=False,
    )
```

time: 62.3 us -> 55.6 us (0.89)
  Pallas kernels: 58.5 us -> 52.4 us
    pallas_call x1, Pallas kernels: 58.5 us -> 52.4 us  [local(): pl.pallas_call(functools.partial(kernel, dets, strips), out_shape=(jax.Sh...]
where the time goes in v3:
time: 55.6 us; the launch traced here: 55.4 us
  Pallas kernels  52.4 us (94%)
  local copies, waits for them, and re-layouts  2.38 us (4%)
  between operations  0.65 us (1%)
    pallas_call x1, Pallas kernels, local(): pl.pallas_call(functools.partial(kernel, dets, strips), out_shape=(jax.Sh...  52.4 us
    unnamed x4, local copies, waits for them, and re-layouts  2.38 us

profile of v3, /device:TPU:0, one launch (start us, length us, event | category | flops | bytes accessed | tf_op | source)
XLA Modules:
  0.0 55.4 jit_solution(2240301111929346300)
XLA Ops:
  0.6 52.4 %shard_map.77 = (f32[1,32,4096]{2,1,0:T(8,128)}, f32[1,37]{1,0:T(1,128)}) custom-call(f32[1,32,4096]{2,1,0:T(8,128)} %sci_ref.1, f32[16,32,256]{2,1,0:T(8,128)} %tmpl_ref.1, f32[12,21]{1,0:T(8,128)} %row_ref.1, f32[12,21]{1,0:T(8,128)} %col_ref.1, s32[1,32]{1,0:T(1,128)} %srow_ref.1, s32[1,32]{1,0:T(1,128)} %scol_ref.1), custom_call_target="tpu_custom_call" | custom-call | tf_op jit(solution)/shard_map/pallas_call | solution.py:466
  53.0 0.0 copy-start
  53.0 1.9 %copy.10 = f32[1,32,4096]{2,1,0:T(8,128)} copy(f32[1,32,4096]{2,1,0:T(8,128)} %get-tuple-element.4) | data formatting | bytes 1048576
  54.9 0.0 copy-done
  54.9 0.5 copy.11
Async XLA Ops:
  53.0 1.9 %copy-start = (f32[1,37]{1,0:T(1,128)S(1)}, f32[1,37]{1,0:T(1,128)}, u32[]{:S(2)}) copy-start(f32[1,37]{1,0:T(1,128)} %get-tuple-element.5) | copy-start | bytes 448

commit v4 on v3

--- a/solution.py
+++ b/solution.py
@@ -83,18 +83,17 @@
     return (sub >= HALO - KH) & (sub < HALO + rows + KH) & (sky >= 0) & (sky < total_rows)
 
 
-def row_stage(sky_ref, row_table_ref, windows, first, count, rows):
+def row_stage(sky_ref, row_table_ref, windows, places, rows):
     size = NB // 2
     lane = iota((2 * HALO + rows, LW), 1)
-    loaded = [pltpu.roll(sky_ref[first + i], KH, 1) for i in range(count + 1)]
-    moved = [jnp.where(lane < KH, loaded[i], loaded[i + 1]) for i in range(count)]
-    moved = jnp.concatenate(moved, axis=1) if count > 1 else moved[0]
+    moved = [pltpu.roll(jnp.where(lane < LW - KH, sky_ref[m + 1], sky_ref[m]), KH, 1) for m in places]
+    moved = jnp.concatenate(moved, axis=1) if len(places) > 1 else moved[0]
     for base, pair in row_filtered(row_table_ref, moved, rows):
         for ref, val in zip(windows, pair):
-            for i in range(count):
+            for i, m in enumerate(places):
                 part = val[:, :, i * LW : (i + 1) * LW]
-                ref[base : base + size, first + i + 1, :, :LW] = part
-                ref[base : base + size, first + i, :, LW:] = part
+                ref[base : base + size, m + 1, :, :LW] = part
+                ref[base : base + size, m, :, LW:] = part
 
 
 def col_stage(windows, col_table_ref, resp_ref, rows, cols):
@@ -386,11 +385,11 @@
     sci_copy.wait()
     for k in range(blocks):
         sci[k] = sci_buf[:, k * LW : (k + 1) * LW]
-    own.wait()
-    for i in range(dets):
-        if i:
-            main_copy(i).wait_recv()
-
+    held = held_rows(LW, first_row, rows, total_rows)
+    windows = (win_hi, win_lo)
+    half = width // LW
+
+    def received(i):
         @pl.when(above)
         def _():
             for p in range(2):
@@ -401,9 +400,24 @@
             for p in range(2):
                 up_copy(i, p).wait_recv()
 
-    held = held_rows(LW, first_row, rows, total_rows)
-    for k in range(blocks):
-        sky[k + 1] = jnp.where(held, frame[:, k * LW : (k + 1) * LW], 0.0)
+        first = half * lax.rem(det + i, dets)
+        for t in range(half):
+            sky[first + t + 1] = jnp.where(held, frame[:, pl.ds(pl.multiple_of((first + t) * LW, LW), LW)], 0.0)
+
+    def place(n):
+        return lax.rem(half * det + 1 + n, blocks + 1)
+
+    def arrive(i, carry):
+        main_copy(i).wait_recv()
+        received(i)
+        row_stage(sky, row_table, windows, [place(half * (i - 1) + t) for t in range(half)], rows)
+        return carry
+
+    own.wait()
+    received(0)
+    lax.fori_loop(1, dets - 1, arrive, 0)
+    main_copy(dets - 1).wait_recv()
+    received(dets - 1)
     stamp_responses(sky, row_table, stamp_table, stamp_win, stamp_resp, scol_ref, rows, cols)
     pack_stamps(stamp_resp, sci, srow_ref, scol_ref, left, right, first_row, rows, cols)
     parts[strip] = normal_part(left, right, maps, rows)
@@ -416,14 +430,10 @@
 
     for i in range(1, strips):
         part_copy(i).start()
-    windows = (win_hi, win_lo)
-
-    def chunk(j, carry):
-        row_stage(sky, row_table, windows, 2 * j, 2, rows)
-        return carry
-
-    lax.fori_loop(0, blocks // 2, chunk, 0)
-    row_stage(sky, row_table, windows, blocks, 1, rows)
+    done = half * (dets - 2)
+    row_stage(sky, row_table, windows, [place(done + t) for t in range(2)], rows)
+    row_stage(sky, row_table, windows, [place(done + 2 + t) for t in range(2)], rows)
+    row_stage(sky, row_table, windows, [place(blocks)], rows)
     col_stage(windows, col_table, resp, rows, cols)
     for i in range(1, strips):
         source = lax.rem(strip + strips - i, strips)

time: 55.6 us -> 52.4 us (0.942); the launches traced: 55.4 us -> 51.6 us
  Pallas kernels: 52.4 us -> 48.5 us
    pallas_call x1, Pallas kernels: 52.4 us -> 48.5 us  [local(): pl.pallas_call(functools.partial(kernel, dets, strips), out_shape=(jax.Sh...]
where the time goes in v4:
time: 52.4 us; the launch traced here: 51.6 us
  Pallas kernels  48.5 us (93%)
  local copies, waits for them, and re-layouts  2.38 us (5%)
  between operations  0.65 us (1%)
    pallas_call x1, Pallas kernels, local(): pl.pallas_call(functools.partial(kernel, dets, strips), out_shape=(jax.Sh...  48.5 us
    unnamed x4, local copies, waits for them, and re-layouts  2.38 us

profile of v4, /device:TPU:0, one launch (start us, length us, event | category | flops | bytes accessed | tf_op | source)
XLA Modules:
  0.0 51.6 jit_solution(10389985823902957051)
XLA Ops:
  0.6 48.5 %shard_map.77 = (f32[1,32,4096]{2,1,0:T(8,128)}, f32[1,37]{1,0:T(1,128)}) custom-call(f32[1,32,4096]{2,1,0:T(8,128)} %sci_ref.1, f32[16,32,256]{2,1,0:T(8,128)} %tmpl_ref.1, f32[12,21]{1,0:T(8,128)} %row_ref.1, f32[12,21]{1,0:T(8,128)} %col_ref.1, s32[1,32]{1,0:T(1,128)} %srow_ref.1, s32[1,32]{1,0:T(1,128)} %scol_ref.1), custom_call_target="tpu_custom_call" | custom-call | tf_op jit(solution)/shard_map/pallas_call | solution.py:476
  49.2 0.0 copy-start
  49.2 1.9 %copy.10 = f32[1,32,4096]{2,1,0:T(8,128)} copy(f32[1,32,4096]{2,1,0:T(8,128)} %get-tuple-element.4) | data formatting | bytes 1048576
  51.0 0.0 copy-done
  51.1 0.5 copy.11
Async XLA Ops:
  49.2 1.9 %copy-start = (f32[1,37]{1,0:T(1,128)S(1)}, f32[1,37]{1,0:T(1,128)}, u32[]{:S(2)}) copy-start(f32[1,37]{1,0:T(1,128)} %get-tuple-element.5) | copy-start | bytes 448

commit v5 on v4

--- a/solution.py
+++ b/solution.py
@@ -278,10 +278,11 @@
 
 def kernel(
     dets, strips,
-    sci_ref, tmpl_ref, row_ref, col_ref, srow_ref, scol_ref,
+    sci_ref, tmpl_ref, row_in, col_in, srow_in, scol_in,
     out_ref, coef_ref,
+    row_ref, col_ref, srow_ref, scol_ref,
     frame, pad, row_table, col_table, stamp_table, win_hi, win_lo, resp, stamp_win, stamp_resp, left, right, maps, parts, sci_buf, sky, sci,
-    main_send, main_recv, up_send, up_recv, down_send, down_recv, part_send, part_recv, own_sem, sci_sem,
+    main_send, main_recv, up_send, up_recv, down_send, down_recv, part_send, part_recv, own_sem, sci_sem, small_sem,
 ):
     _, rows, cols = sci_ref.shape
     width = tmpl_ref.shape[2]
@@ -289,6 +290,13 @@
     det, strip = lax.axis_index("det"), lax.axis_index("strip")
     above, below = strip > 0, strip < strips - 1
     first_row = strip * rows
+
+    small = [
+        pltpu.make_async_copy(a, b, small_sem.at[i])
+        for i, (a, b) in enumerate(((row_in, row_ref), (col_in, col_ref), (srow_in, srow_ref), (scol_in, scol_ref)))
+    ]
+    for copy in small:
+        copy.start()
 
     barrier = pltpu.get_barrier_semaphore()
 
@@ -379,6 +387,8 @@
     sky[0] = jnp.zeros((2 * HALO + rows, LW), F32)
     sky[blocks + 1] = jnp.zeros((2 * HALO + rows, LW), F32)
     sci[blocks] = jnp.zeros((rows, LW), F32)
+    for copy in small:
+        copy.wait()
     build_row_table(row_ref, pad, row_table, rows)
     build_col_tables(col_ref, pad, col_table, stamp_table)
     build_maps(maps, first_row, rows, total_rows)
@@ -471,14 +481,19 @@
     packed = stamps // 2 * LW
     any_space = pl.BlockSpec(memory_space=pl.ANY)
     vmem = pl.BlockSpec(memory_space=pltpu.VMEM)
-    smem = pl.BlockSpec(memory_space=pltpu.SMEM)
+    hbm = pl.BlockSpec(memory_space=pltpu.HBM)
     dma = pltpu.SemaphoreType.DMA
+    results = (jax.ShapeDtypeStruct(science.shape, F32), jax.ShapeDtypeStruct((1, NU), F32))
     return pl.pallas_call(
         functools.partial(kernel, dets, strips),
-        out_shape=(jax.ShapeDtypeStruct(science.shape, F32), jax.ShapeDtypeStruct((1, NU), F32)),
-        in_specs=[any_space, any_space, vmem, vmem, smem, smem],
+        out_shape=(pltpu.VMEM(science.shape, F32), pltpu.VMEM((1, NU), F32)),
+        in_specs=[hbm] * 6,
         out_specs=(vmem, vmem),
         scratch_shapes=[
+            pltpu.VMEM((NB, KS), F32),
+            pltpu.VMEM((NB, KS), F32),
+            pltpu.SMEM((1, stamps), jnp.int32),
+            pltpu.SMEM((1, stamps), jnp.int32),
             pltpu.VMEM((rows + 2 * HALO, cols), F32),
             pltpu.VMEM((16, LW), F32),
             pltpu.VMEM((NB * rows, 256), BF),
@@ -497,12 +512,16 @@
             pltpu.VMEM((blocks + 2, rows + 2 * HALO, LW), F32),
             pltpu.VMEM((blocks + 1, rows, LW), F32),
             dma((dets,)), dma((dets,)), dma((2, dets)), dma((2, dets)), dma((2, dets)), dma((2, dets)),
-            dma((strips,)), dma((strips,)), dma, dma,
+            dma((strips,)), dma((strips,)), dma, dma, dma((4,)),
         ],
         compiler_params=pltpu.CompilerParams(
-            collective_id=0, has_side_effects=True, vmem_limit_bytes=56 * 1024 * 1024
+            collective_id=0, has_side_effects=True, vmem_limit_bytes=53 * 1024 * 1024
         ),
-    )(science, template, row_taps, col_taps, stamp_rows, stamp_cols)
+    )(
+        science,
+        template,
+        *[pltpu.with_memory_space_constraint(v, pltpu.HBM) for v in (row_taps, col_taps, stamp_rows, stamp_cols)],
+    )
 
 
 def solution(mesh):

time: 52.4 us -> 49.7 us (0.948)
  Pallas kernels: 48.5 us -> 47 us
  local copies, waits for them, and re-layouts: 2.38 us -> 1.31 us
    pallas_call x1, Pallas kernels: 48.5 us -> 47 us  [local(): pl.pallas_call(functools.partial(kernel, dets, strips), out_shape=(pltpu....]
    unnamed x4 -> x2, local copies, waits for them, and re-layouts: 2.38 us -> 1.31 us
where the time goes in v5:
time: 49.7 us; the launch traced here: 48.9 us
  Pallas kernels  47 us (95%)
  local copies, waits for them, and re-layouts  1.31 us (3%)
  between operations  0.64 us (1%)
    pallas_call x1, Pallas kernels, local(): pl.pallas_call(functools.partial(kernel, dets, strips), out_shape=(pltpu....  47 us
    unnamed x2, local copies, waits for them, and re-layouts  1.31 us

profile of v5, /device:TPU:0, one launch (start us, length us, event | category | flops | bytes accessed | tf_op | source)
XLA Modules:
  0.0 48.9 jit_solution(14534515339465503004)
XLA Ops:
  0.6 47.0 %shard_map.77 = (f32[1,32,4096]{2,1,0:T(8,128)S(1)}, f32[1,37]{1,0:T(1,128)S(1)}) custom-call(f32[1,32,4096]{2,1,0:T(8,128)} %sci_ref.1, f32[16,32,256]{2,1,0:T(8,128)} %tmpl_ref.1, f32[12,21]{1,0:T(8,128)} %row_in.1, f32[12,21]{1,0:T(8,128)} %col_in.1, s32[1,32]{1,0:T(1,128)} %srow_in.1, s32[1,32]{1,0:T(1,128)} %scol_in.1), custom_call_target="tpu_custom_call" | custom-call | tf_op jit(solution)/shard_map/pallas_call | solution.py:487
  47.6 0.8 %copy.10 = f32[1,32,4096]{2,1,0:T(8,128)} copy(f32[1,32,4096]{2,1,0:T(8,128)S(1)} %get-tuple-element.2) | data formatting | bytes 1048576
  48.4 0.5 %copy.11 = f32[1,37]{1,0:T(1,128)} copy(f32[1,37]{1,0:T(1,128)S(1)} %get-tuple-element.3) | data formatting | bytes 296

commit v6 on v5

--- a/solution.py
+++ b/solution.py
@@ -108,7 +108,7 @@
             resp_ref[b, k : k + per] = (out[:, :LW] + out[:, LW:]).reshape(per, rows, LW)
         return carry
 
-    lax.fori_loop(0, NB, body, 0)
+    lax.fori_loop(0, NB, body, 0, unroll=True)
 
 
 def gather(ref, starts):
@@ -139,14 +139,14 @@
                     win_ref[base : base + size, 2 * u + i, :, part * LW : (part + 1) * LW] = val[:, :, i * LW : (i + 1) * LW]
         return carry
 
-    lax.fori_loop(0, pairs // 2, body, 0)
+    lax.fori_loop(0, pairs // 2, body, 0, unroll=True)
 
     def filt(b, carry):
         out = jnp.dot(win_ref[b].reshape(pairs * rows, 2 * LW), stamp_table_ref[b], preferred_element_type=F32)
         resp_ref[b] = (out[:, :LW] + out[:, LW:]).reshape(pairs, rows, LW)
         return carry
 
-    lax.fori_loop(0, NB, filt, 0)
+    lax.fori_loop(0, NB, filt, 0, unroll=True)
 
 
 def pack_stamps(resp_ref, sci_ref, rows_ref, cols_ref, left_ref, right_ref, first_row, rows, cols):
@@ -179,7 +179,7 @@
                 left_ref[g, (m + 3) * PLANES * 8 : (m + 4) * PLANES * 8, pl.ds(at, LW)] = low
         return carry
 
-    lax.fori_loop(0, resp_ref.shape[1], body, 0)
+    lax.fori_loop(0, resp_ref.shape[1], body, 0, unroll=4)
 
 
 def build_maps(maps_ref, first_row, rows, total_rows):

time: 49.7 us -> 45.8 us (0.922)
  Pallas kernels: 47 us -> 43.1 us
    pallas_call x1, Pallas kernels: 47 us -> 43.1 us  [local(): pl.pallas_call(functools.partial(kernel, dets, strips), out_shape=(pltpu....]
where the time goes in v6:
time: 45.8 us; the launch traced here: 45.1 us
  Pallas kernels  43.1 us (94%)
  local copies, waits for them, and re-layouts  1.31 us (3%)
  between operations  0.64 us (1%)
    pallas_call x1, Pallas kernels, local(): pl.pallas_call(functools.partial(kernel, dets, strips), out_shape=(pltpu....  43.1 us
    unnamed x2, local copies, waits for them, and re-layouts  1.31 us

profile of v6, /device:TPU:0, one launch (start us, length us, event | category | flops | bytes accessed | tf_op | source)
XLA Modules:
  0.0 45.1 jit_solution(14178931855815233197)
XLA Ops:
  0.6 43.1 %shard_map.77 = (f32[1,32,4096]{2,1,0:T(8,128)S(1)}, f32[1,37]{1,0:T(1,128)S(1)}) custom-call(f32[1,32,4096]{2,1,0:T(8,128)} %sci_ref.1, f32[16,32,256]{2,1,0:T(8,128)} %tmpl_ref.1, f32[12,21]{1,0:T(8,128)} %row_in.1, f32[12,21]{1,0:T(8,128)} %col_in.1, s32[1,32]{1,0:T(1,128)} %srow_in.1, s32[1,32]{1,0:T(1,128)} %scol_in.1), custom_call_target="tpu_custom_call" | custom-call | tf_op jit(solution)/shard_map/pallas_call | solution.py:487
  43.8 0.8 %copy.10 = f32[1,32,4096]{2,1,0:T(8,128)} copy(f32[1,32,4096]{2,1,0:T(8,128)S(1)} %get-tuple-element.2) | data formatting | bytes 1048576
  44.6 0.5 %copy.11 = f32[1,37]{1,0:T(1,128)} copy(f32[1,37]{1,0:T(1,128)S(1)} %get-tuple-element.3) | data formatting | bytes 296

commit v7 on v6

--- a/solution.py
+++ b/solution.py
@@ -195,7 +195,10 @@
         y = (2.0 / total_rows) * (first_row + 8 * g + lax.rem(iota((span, LW), 0), 8)).astype(F32) - 1.0
         level = plain + jnp.where(real & (kind == 2), y, zero)
         for i, part in enumerate((level, in_x, level * y, in_x * y)):
-            maps_ref[g * span : (g + 1) * span, i * LW : (i + 1) * LW] = part
+            high, low = split(part)
+            maps_ref[g * span : (g + 1) * span, i * LW : (i + 1) * LW] = high
+            if i == 2:
+                maps_ref[g * span : (g + 1) * span, 4 * LW :] = low
 
 
 def normal_part(left_ref, right_ref, maps_ref, rows):
@@ -206,17 +209,25 @@
         out = lax.dot_general(left_ref[g], right_ref[g], (((1,), (1,)), ((), ())), preferred_element_type=F32)
         folded = out[: 3 * span, :span] + out[: 3 * span, span:] + out[3 * span :, :span]
         picked.append(jnp.sum(folded.reshape(3 * PLANES, 8, span) * same_y[None], axis=1))
-    total = jnp.dot(
-        jnp.concatenate(picked, axis=1), maps_ref[...], precision=HIGHEST_MODE, preferred_element_type=F32
-    )
-    return jnp.concatenate(
+    sums = jnp.concatenate(picked, axis=1)
+    high, low = split(sums)
+    lower = (sums - high.astype(F32) - low.astype(F32)).astype(BF)
+    total = jnp.dot(jnp.concatenate([high, low, lower], axis=0), maps_ref[...], preferred_element_type=F32)
+    total = total[:48] + total[48:96] + total[96:]
+    squared = total[:, 2 * LW : 3 * LW] + total[:, 4 * LW :]
+    whole = jnp.concatenate(
         [
             total[0:16, 0:LW] + total[16:32, LW : 2 * LW],
             total[16:32, 0:LW] + total[32:48, LW : 2 * LW],
-            total[0:16, 2 * LW : 3 * LW] + total[16:32, 3 * LW :],
+            squared[0:16] + total[16:32, 3 * LW : 4 * LW],
         ],
         axis=0,
     )
+    return jnp.where(iota((24, LW), 1) < LW // 2, whole[:24], pltpu.roll(whole[24:], LW // 2, 1))
+
+
+def unfolded(halves):
+    return jnp.concatenate([halves, pltpu.roll(halves, LW // 2, 1)], axis=0)
 
 
 PIVOTS = [*range(0, 13), *range(16, 28), *range(32, 44)]
@@ -469,7 +480,7 @@
     normal = parts[0]
     for i in range(1, strips):
         normal = normal + parts[i]
-    answer = solve(normal)
+    answer = solve(unfolded(normal))
     coef_ref[...] = coeff_row(answer)[:, :NU]
     apply_model(answer, resp, sci, out_ref, first_row, rows, total_rows, cols)
 
@@ -506,8 +517,8 @@
             pltpu.VMEM((NB, stamps // 2, rows, LW), F32),
             pltpu.VMEM((rows // 8, 6 * PLANES * 8, packed), BF),
             pltpu.VMEM((rows // 8, 2 * PLANES * 8, packed), BF),
-            pltpu.VMEM((rows * PLANES, 4 * LW), F32),
-            pltpu.VMEM((strips, 48, LW), F32),
+            pltpu.VMEM((rows * PLANES, 5 * LW), BF),
+            pltpu.VMEM((strips, 24, LW), F32),
             pltpu.VMEM((rows, cols), F32),
             pltpu.VMEM((blocks + 2, rows + 2 * HALO, LW), F32),
             pltpu.VMEM((blocks + 1, rows, LW), F32),

time: 45.8 us -> 45 us (0.983)
  Pallas kernels: 43.1 us -> 42.4 us
    pallas_call x1, Pallas kernels: 43.1 us -> 42.4 us  [local(): pl.pallas_call(functools.partial(kernel, dets, strips), out_shape=(pltpu....]
where the time goes in v7:
time: 45 us; the launch traced here: 44.4 us
  Pallas kernels  42.4 us (94%)
  local copies, waits for them, and re-layouts  1.31 us (3%)
  between operations  0.64 us (1%)
    pallas_call x1, Pallas kernels, local(): pl.pallas_call(functools.partial(kernel, dets, strips), out_shape=(pltpu....  42.4 us
    unnamed x2, local copies, waits for them, and re-layouts  1.31 us

profile of v7, /device:TPU:0, one launch (start us, length us, event | category | flops | bytes accessed | tf_op | source)
XLA Modules:
  0.0 44.4 jit_solution(1406516245193144491)
XLA Ops:
  0.6 42.4 %shard_map.77 = (f32[1,32,4096]{2,1,0:T(8,128)S(1)}, f32[1,37]{1,0:T(1,128)S(1)}) custom-call(f32[1,32,4096]{2,1,0:T(8,128)} %sci_ref.1, f32[16,32,256]{2,1,0:T(8,128)} %tmpl_ref.1, f32[12,21]{1,0:T(8,128)} %row_in.1, f32[12,21]{1,0:T(8,128)} %col_in.1, s32[1,32]{1,0:T(1,128)} %srow_in.1, s32[1,32]{1,0:T(1,128)} %scol_in.1), custom_call_target="tpu_custom_call" | custom-call | tf_op jit(solution)/shard_map/pallas_call | solution.py:498
  43.1 0.8 %copy.10 = f32[1,32,4096]{2,1,0:T(8,128)} copy(f32[1,32,4096]{2,1,0:T(8,128)S(1)} %get-tuple-element.2) | data formatting | bytes 1048576
  43.9 0.5 %copy.11 = f32[1,37]{1,0:T(1,128)} copy(f32[1,37]{1,0:T(1,128)S(1)} %get-tuple-element.3) | data formatting | bytes 296

commit v8 on v7

--- a/solution.py
+++ b/solution.py
@@ -238,16 +238,29 @@
     live = (lax.rem(sub, 16) < NB) | (sub == ONE_PLANE)
     mat = jnp.where((sub == lane) & live, normal + RIDGE_WEIGHT, normal)
     at = lambda value, k: value[k : k + 1, :]
-    for i in range(0, NU - 1, 2):
-        j, k = PIVOTS[i], PIVOTS[i + 1]
-        cj = jnp.broadcast_to(mat[:, j : j + 1], (48, LW))
-        ck = jnp.broadcast_to(mat[:, k : k + 1], (48, LW))
-        jj, jk, kj, kk = at(cj, j), at(ck, j), at(cj, k), at(ck, k)
-        scale = 1.0 / (jj * kk - jk * kj)
-        rj, rk = at(mat, j), at(mat, k)
-        nj = (kk * rj - jk * rk) * scale
-        nk = (jj * rk - kj * rj) * scale
-        mat = jnp.where(sub == j, nj, jnp.where(sub == k, nk, mat - cj * nj - ck * nk))
+
+    def pair(first, second, tops, lows):
+        scale = 1.0 / (first[0] * second[1] - first[1] * second[0])
+        return [
+            ((second[1] * t - first[1] * w) * scale, (first[0] * w - second[0] * t) * scale) for t, w in zip(tops, lows)
+        ]
+
+    for i in range(0, NU - 1, 4):
+        picks = PIVOTS[i : i + 4]
+        columns = [jnp.broadcast_to(mat[:, k : k + 1], (48, LW)) for k in picks]
+        rows = [[at(c, k) for c in columns] + [at(mat, k)] for k in picks]
+        upper = pair(rows[0], rows[1], rows[0][2:], rows[1][2:])
+        rest = [[r[2 + j] - r[0] * t - r[1] * w for j, (t, w) in enumerate(upper)] for r in rows[2:]]
+        ((third, fourth),) = pair(rest[0], rest[1], rest[0][2:], rest[1][2:])
+        first = upper[2][0] - upper[0][0] * third - upper[1][0] * fourth
+        second = upper[2][1] - upper[0][1] * third - upper[1][1] * fourth
+        solved = [first, second, third, fourth]
+        left = mat
+        for c, r in zip(columns, solved):
+            left = left - c * r
+        for k, r in zip(picks, solved):
+            left = jnp.where(sub == k, r, left)
+        mat = left
     k = PIVOTS[-1]
     column = jnp.broadcast_to(mat[:, k : k + 1], (48, LW))
     row = at(mat, k) / at(column, k)

time: 45 us -> 44.5 us (0.989)
  Pallas kernels: 42.4 us -> 41.9 us
    pallas_call x1, Pallas kernels: 42.4 us -> 41.9 us  [local(): pl.pallas_call(functools.partial(kernel, dets, strips), out_shape=(pltpu....]
where the time goes in v8:
time: 44.5 us; the launch traced here: 43.9 us
  Pallas kernels  41.9 us (94%)
  local copies, waits for them, and re-layouts  1.31 us (3%)
  between operations  0.64 us (1%)
    pallas_call x1, Pallas kernels, local(): pl.pallas_call(functools.partial(kernel, dets, strips), out_shape=(pltpu....  41.9 us
    unnamed x2, local copies, waits for them, and re-layouts  1.31 us

profile of v8, /device:TPU:0, one launch (start us, length us, event | category | flops | bytes accessed | tf_op | source)
XLA Modules:
  0.0 43.9 jit_solution(2021824000847052414)
XLA Ops:
  0.6 41.9 %shard_map.77 = (f32[1,32,4096]{2,1,0:T(8,128)S(1)}, f32[1,37]{1,0:T(1,128)S(1)}) custom-call(f32[1,32,4096]{2,1,0:T(8,128)} %sci_ref.1, f32[16,32,256]{2,1,0:T(8,128)} %tmpl_ref.1, f32[12,21]{1,0:T(8,128)} %row_in.1, f32[12,21]{1,0:T(8,128)} %col_in.1, s32[1,32]{1,0:T(1,128)} %srow_in.1, s32[1,32]{1,0:T(1,128)} %scol_in.1), custom_call_target="tpu_custom_call" | custom-call | tf_op jit(solution)/shard_map/pallas_call | solution.py:511
  42.6 0.8 %copy.10 = f32[1,32,4096]{2,1,0:T(8,128)} copy(f32[1,32,4096]{2,1,0:T(8,128)S(1)} %get-tuple-element.2) | data formatting | bytes 1048576
  43.4 0.5 %copy.11 = f32[1,37]{1,0:T(1,128)} copy(f32[1,37]{1,0:T(1,128)S(1)} %get-tuple-element.3) | data formatting | bytes 296

commit v9 on v8

--- a/solution.py
+++ b/solution.py
@@ -16,6 +16,7 @@
 HALO = 16
 SLOT = 64
 PLANES = 16
+FITTED = 14
 ONE_PLANE = 12
 SCI_PLANE = 13
 RIDGE_WEIGHT = 1.0
@@ -112,6 +113,7 @@
 
 
 def gather(ref, starts):
+    tall = 3 * FITTED * 8
     picked = []
     for t, start in enumerate(starts):
         k = start // LW
@@ -170,13 +172,13 @@
             high, low = split(planes.reshape(PLANES * 8, LW))
             right_ref[g, : PLANES * 8, pl.ds(at, LW)] = high
             right_ref[g, PLANES * 8 :, pl.ds(at, LW)] = low
-            moment = planes * hit[None]
+            moment = planes[:FITTED] * hit[None]
             for m in range(3):
                 if m:
                     moment = moment * xv[None]
-                high, low = split(moment.reshape(PLANES * 8, LW))
-                left_ref[g, m * PLANES * 8 : (m + 1) * PLANES * 8, pl.ds(at, LW)] = high
-                left_ref[g, (m + 3) * PLANES * 8 : (m + 4) * PLANES * 8, pl.ds(at, LW)] = low
+                high, low = split(moment.reshape(FITTED * 8, LW))
+                left_ref[g, m * FITTED * 8 : (m + 1) * FITTED * 8, pl.ds(at, LW)] = high
+                left_ref[g, (m + 3) * FITTED * 8 : (m + 4) * FITTED * 8, pl.ds(at, LW)] = low
         return carry
 
     lax.fori_loop(0, resp_ref.shape[1], body, 0, unroll=4)
@@ -204,12 +206,15 @@
 def normal_part(left_ref, right_ref, maps_ref, rows):
     span = PLANES * 8
     same_y = (lax.rem(iota((8, span), 1), 8) == iota((8, span), 0)).astype(F32)
+    tall = 3 * FITTED * 8
     picked = []
     for g in range(rows // 8):
         out = lax.dot_general(left_ref[g], right_ref[g], (((1,), (1,)), ((), ())), preferred_element_type=F32)
-        folded = out[: 3 * span, :span] + out[: 3 * span, span:] + out[3 * span :, :span]
-        picked.append(jnp.sum(folded.reshape(3 * PLANES, 8, span) * same_y[None], axis=1))
+        folded = out[:tall, :span] + out[:tall, span:] + out[tall:, :span]
+        picked.append(jnp.sum(folded.reshape(3 * FITTED, 8, span) * same_y[None], axis=1))
     sums = jnp.concatenate(picked, axis=1)
+    gap = jnp.zeros((PLANES - FITTED, sums.shape[1]), F32)
+    sums = jnp.concatenate([v for m in range(3) for v in (sums[m * FITTED : (m + 1) * FITTED], gap)], axis=0)
     high, low = split(sums)
     lower = (sums - high.astype(F32) - low.astype(F32)).astype(BF)
     total = jnp.dot(jnp.concatenate([high, low, lower], axis=0), maps_ref[...], preferred_element_type=F32)
@@ -528,7 +533,7 @@
             pltpu.VMEM((NB, blocks, rows, LW), F32),
             pltpu.VMEM((NB, stamps // 2, rows, 256), BF),
             pltpu.VMEM((NB, stamps // 2, rows, LW), F32),
-            pltpu.VMEM((rows // 8, 6 * PLANES * 8, packed), BF),
+            pltpu.VMEM((rows // 8, 6 * FITTED * 8, packed), BF),
             pltpu.VMEM((rows // 8, 2 * PLANES * 8, packed), BF),
             pltpu.VMEM((rows * PLANES, 5 * LW), BF),
             pltpu.VMEM((strips, 24, LW), F32),

time: 44.5 us -> 43.7 us (0.982)
  Pallas kernels: 41.9 us -> 41.1 us
    pallas_call x1, Pallas kernels: 41.9 us -> 41.1 us  [local(): pl.pallas_call(functools.partial(kernel, dets, strips), out_shape=(pltpu....]
where the time goes in v9:
time: 43.7 us; the launch traced here: 43 us
  Pallas kernels  41.1 us (94%)
  local copies, waits for them, and re-layouts  1.31 us (3%)
  between operations  0.64 us (1%)
    pallas_call x1, Pallas kernels, local(): pl.pallas_call(functools.partial(kernel, dets, strips), out_shape=(pltpu....  41.1 us
    unnamed x2, local copies, waits for them, and re-layouts  1.31 us

profile of v9, /device:TPU:0, one launch (start us, length us, event | category | flops | bytes accessed | tf_op | source)
XLA Modules:
  0.0 43.0 jit_solution(12841355049691743452)
XLA Ops:
  0.6 41.1 %shard_map.77 = (f32[1,32,4096]{2,1,0:T(8,128)S(1)}, f32[1,37]{1,0:T(1,128)S(1)}) custom-call(f32[1,32,4096]{2,1,0:T(8,128)} %sci_ref.1, f32[16,32,256]{2,1,0:T(8,128)} %tmpl_ref.1, f32[12,21]{1,0:T(8,128)} %row_in.1, f32[12,21]{1,0:T(8,128)} %col_in.1, s32[1,32]{1,0:T(1,128)} %srow_in.1, s32[1,32]{1,0:T(1,128)} %scol_in.1), custom_call_target="tpu_custom_call" | custom-call | tf_op jit(solution)/shard_map/pallas_call | solution.py:516
  41.7 0.8 %copy.10 = f32[1,32,4096]{2,1,0:T(8,128)} copy(f32[1,32,4096]{2,1,0:T(8,128)S(1)} %get-tuple-element.2) | data formatting | bytes 1048576
  42.5 0.5 %copy.11 = f32[1,37]{1,0:T(1,128)} copy(f32[1,37]{1,0:T(1,128)S(1)} %get-tuple-element.3) | data formatting | bytes 296

commit v10 on v9

--- a/solution.py
+++ b/solution.py
@@ -326,6 +326,13 @@
     ]
     for copy in small:
         copy.start()
+    here = pl.ds(pl.multiple_of(det * width, width), width)
+    own = pltpu.make_async_copy(
+        tmpl_ref.at[det], frame.at[pl.ds(HALO, rows), here], own_sem
+    )
+    own.start()
+    sci_copy = pltpu.make_async_copy(sci_ref.at[0], sci_buf, sci_sem)
+    sci_copy.start()
 
     barrier = pltpu.get_barrier_semaphore()
 
@@ -364,7 +371,6 @@
     count = (dets - 1) + dets * (2 - ends) + (strips - 3 + ends)
     pl.semaphore_wait(barrier, count)
 
-    here = pl.ds(pl.multiple_of(det * width, width), width)
 
     def main_copy(i):
         target = lax.rem(det + dets - i, dets)
@@ -392,12 +398,6 @@
             down_send.at[p, i], down_recv.at[p, i], device_id=(target, strip + 1), device_id_type=MESH,
         )
 
-    own = pltpu.make_async_copy(
-        tmpl_ref.at[det], frame.at[pl.ds(HALO, rows), here], own_sem
-    )
-    own.start()
-    sci_copy = pltpu.make_async_copy(sci_ref.at[0], sci_buf, sci_sem)
-    sci_copy.start()
     for i in range(dets):
         if i:
             main_copy(i).start()

time: 43.7 us -> 43.7 us (level)
  no operation moved by 1% of the time
where the time goes in v10:
time: 43.7 us; the launch traced here: 43.1 us
  Pallas kernels  41.1 us (94%)
  local copies, waits for them, and re-layouts  1.31 us (3%)
  between operations  0.64 us (1%)
    pallas_call x1, Pallas kernels, local(): pl.pallas_call(functools.partial(kernel, dets, strips), out_shape=(pltpu....  41.1 us
    unnamed x2, local copies, waits for them, and re-layouts  1.31 us

profile of v10, /device:TPU:0, one launch (start us, length us, event | category | flops | bytes accessed | tf_op | source)
XLA Modules:
  0.0 43.1 jit_solution(17484408739095438954)
XLA Ops:
  0.6 41.1 %shard_map.77 = (f32[1,32,4096]{2,1,0:T(8,128)S(1)}, f32[1,37]{1,0:T(1,128)S(1)}) custom-call(f32[1,32,4096]{2,1,0:T(8,128)} %sci_ref.1, f32[16,32,256]{2,1,0:T(8,128)} %tmpl_ref.1, f32[12,21]{1,0:T(8,128)} %row_in.1, f32[12,21]{1,0:T(8,128)} %col_in.1, s32[1,32]{1,0:T(1,128)} %srow_in.1, s32[1,32]{1,0:T(1,128)} %scol_in.1), custom_call_target="tpu_custom_call" | custom-call | tf_op jit(solution)/shard_map/pallas_call | solution.py:516
  41.7 0.8 %copy.10 = f32[1,32,4096]{2,1,0:T(8,128)} copy(f32[1,32,4096]{2,1,0:T(8,128)S(1)} %get-tuple-element.2) | data formatting | bytes 1048576
  42.5 0.5 %copy.11 = f32[1,37]{1,0:T(1,128)} copy(f32[1,37]{1,0:T(1,128)S(1)} %get-tuple-element.3) | data formatting | bytes 296
